TPU v7x, 32 devices: a whole 2x2x4 slice. The times are simulated.
32 devices in a mesh: player: 2 (over x), feat: 16 (over z, y, core).
Axes of the slice: x: 2, y: 2, z: 4, core: 2. Of those that a mesh axis runs over, the one named last changes fastest.
Arguments:
- slab: bfloat16 [128, 524288], P(None, 'feat'), may hold values from -16 to 16
- players: bfloat16 [512, 524288], P('player', 'feat'), may hold values from -16 to 16
Outputs:
- updated: bfloat16 [512, 524288], P('player', 'feat')
All inputs are finite; a program needn't handle non-finite values.
Results may differ from a plain program's by a relative error of at most 0.0083.
Values may be sent and summed in bfloat16 or wider, within the bound.
No kernel may reach another device: no remote copies, remote signals or barrier semaphores. Data moves between devices by JAX's collectives and lax.ppermute only.
A program may use at most 192 MiB of HBM per device.

v0:
```python
import jax
import jax.numpy as jnp
from jax import lax
from jax.sharding import PartitionSpec as P

F = 524288
STEPS = 2


def on_device(slab, players):
    own_count = players.shape[0]
    k_total = own_count * lax.axis_size("player")
    first = lax.axis_index("player") * own_count
    inverse_square = 1.0 / F / F
    rows = jnp.arange(k_total, dtype=jnp.int32)[:, None]
    cols = first + jnp.arange(own_count, dtype=jnp.int32)[None, :]
    weights = players
    for step in range(STEPS):
        partial_proj = lax.dot_general(
            weights, slab, (((1,), (1,)), ((), ())), preferred_element_type=jnp.float32
        )
        proj_own = lax.psum(partial_proj, "feat")
        proj_all = lax.all_gather(proj_own, "player", axis=0, tiled=True)
        scaled = (proj_own / F).astype(jnp.bfloat16)
        reward = jnp.dot(scaled, slab, preferred_element_type=jnp.float32)
        correlation = (
            lax.dot_general(
                proj_all, proj_own, (((1,), (1,)), ((), ())), precision=lax.Precision.HIGHEST
            )
            * inverse_square
        )
        coeff = jnp.where(rows < cols, correlation, jnp.zeros_like(correlation)).astype(
            jnp.bfloat16
        )
        penalty = lax.dot_general(
            coeff,
            lax.all_gather(weights, "player", axis=0, tiled=True),
            (((0,), (0,)), ((), ())),
            preferred_element_type=jnp.float32,
        )
        update = weights.astype(jnp.float32) + reward - penalty
        squares = jnp.sum(update * update, axis=1)
        total = lax.psum(squares, "feat")
        weights = (update * jnp.sqrt(F / (total + 1e-06))[:, None]).astype(jnp.bfloat16)
    return weights


def solution(mesh):
    in_specs = (P(None, "feat"), P("player", "feat"))
    out_specs = P("player", "feat")
    return jax.shard_map(
        on_device, mesh=mesh, in_specs=in_specs, out_specs=out_specs, check_vma=False
    )
```

profile of v0, /device:TPU:0, one launch (start us, length us, event | category | flops | bytes accessed | tf_op | source)
XLA Modules:
  0.0 997.6 jit_solution(13927933309180599819)
XLA Ops:
  7.4 13.3 %fusion.8 = f32[256,128]{1,0:T(8,128)} fusion(bf16[256,32768]{1,0:T(8,128)(2,1)} %param.3, bf16[128,32768]{1,0:T(8,128)(2,1)} %param.2), kind=kOutput, calls=%fused_computation.24 | convolution fusion | flops 2147483648 | bytes 25296896 | tf_op jit(solution)/shard_map/dot_general | solution.py:19
  20.7 0.0 all-gather.3.cloned.1.call-start
  20.7 0.5 all-gather.3.cloned.1.call-update
  21.3 0.0 all-reduce.5.cloned.1.call-start
  21.3 90.4 %all-reduce.3.cloned.1.call-done = f32[256,128]{1,0:T(8,128)} async-done(((f32[256,128]{1,0:T(8,128)}), f32[256,128]{1,0:T(8,128)}) %all-reduce.3.cloned.1.call-update) | async-done | bytes 131088 | tf_op jit(solution)/shard_map/psum | solution.py:22
  111.7 10.1 %all_gather.12 = f32[512,128]{1,0:T(8,128)S(1)} all-gather(f32[256,128]{1,0:T(8,128)} %all-reduce.3.cloned.1.call-done), channel_id=1, replica_groups=mesh['player'=2,'feat'=16] {'player'}, dimensions={0}, use_global_device_ids=true | all-gather | bytes 393216 | tf_op jit(solution)/shard_map/all_gather | solution.py:23
  121.8 1.5 fusion.2
  123.3 23.8 %convolution_add_fusion.1 = f32[256,32768]{1,0:T(8,128)} fusion(bf16[128,32768]{1,0:T(8,128)(2,1)} %param.2, bf16[256,32768]{1,0:T(8,128)(2,1)} %param.3, f32[256,128]{1,0:T(8,128)} %all-reduce.3.cloned.1.call-done), kind=kOutput, calls=%fused_computation.3 | convolution fusion | flops 2164326400 | bytes 58851328 | tf_op jit(solution)/shard_map/dot_general | solution.py:25
  147.1 269.6 %all-gather.3.cloned.1.call-done = bf16[512,32768]{1,0:T(8,128)(2,1)} async-done(((bf16[256,32768]{1,0:T(8,128)(2,1)}), bf16[512,32768]{1,0:T(8,128)(2,1)}) %all-gather.3.cloned.1.call-update) | async-done | bytes 33554448 | tf_op jit(solution)/shard_map/all_gather | solution.py:37
  416.7 34.8 %multiply_reduce_fusion.1 = (f32[256]{0:T(256)S(1)}, f32[256,32768]{1,0:T(8,128)}) fusion(f32[256,32768]{1,0:T(8,128)} %convolution_add_fusion.1, bf16[512,256]{1,0:T(8,128)(2,1)S(1)} %fusion.2, bf16[512,32768]{1,0:T(8,128)(2,1)} %all-gather.3.cloned.1.call-done), kind=kOutput, calls=%fused_computation.7 | convolution fusion | flops 8615100416 | bytes 100926464 | tf_op jit(solution)/shard_map/dot_general | solution.py:35
  451.5 33.1 %psum.29 = f32[256]{0:T(256)S(1)} all-reduce(f32[256]{0:T(256)S(1)} %get-tuple-element.5), channel_id=1, replica_groups=mesh['player'=2,'feat'=16] {'feat'}, use_global_device_ids=true, to_apply=%region_2.3 | all-reduce | flops 256 | bytes 2048 | tf_op jit(solution)/shard_map/psum | solution.py:43
  484.6 17.5 %multiply_convert_fusion.1 = bf16[256,32768]{1,0:T(8,128)(2,1)} fusion(f32[256,32768]{1,0:T(8,128)} %get-tuple-element.6, f32[256]{0:T(256)S(1)} %divide_sqrt_fusion.1), kind=kLoop, calls=%fused_computation.6 | loop fusion | flops 16777216 | bytes 50332672 | tf_op jit(solution)/shard_map/convert_element_type | solution.py:44
  502.1 13.3 %fusion.9 = f32[256,128]{1,0:T(8,128)} fusion(bf16[256,32768]{1,0:T(8,128)(2,1)} %multiply_convert_fusion.1, bf16[128,32768]{1,0:T(8,128)(2,1)} %param.2), kind=kOutput, calls=%fused_computation.25 | convolution fusion | flops 2147483648 | bytes 25296896 | tf_op jit(solution)/shard_map/dot_general | solution.py:19
  515.4 0.0 all-reduce.5.cloned.1.call-update
  515.4 0.0 all-gather.5.cloned.1.call-start
  515.4 0.5 all-gather.5.cloned.1.call-update
  516.0 84.2 %all-reduce.5.cloned.1.call-done = f32[256,128]{1,0:T(8,128)} async-done(((f32[256,128]{1,0:T(8,128)}), f32[256,128]{1,0:T(8,128)}) %all-reduce.5.cloned.1.call-update) | async-done | bytes 131088 | tf_op jit(solution)/shard_map/psum | solution.py:22
  600.1 9.9 all_gather.14
  610.0 1.5 fusion.3
  611.5 23.8 %convolution_add_fusion = f32[256,32768]{1,0:T(8,128)} fusion(bf16[128,32768]{1,0:T(8,128)(2,1)} %param.2, bf16[256,32768]{1,0:T(8,128)(2,1)} %multiply_convert_fusion.1, f32[256,128]{1,0:T(8,128)} %all-reduce.5.cloned.1.call-done), kind=kOutput, calls=%fused_computation.1 | convolution fusion | flops 2164326400 | bytes 58851328 | tf_op jit(solution)/shard_map/dot_general | solution.py:25
  635.3 269.7 %all-gather.5.cloned.1.call-done = bf16[512,32768]{1,0:T(8,128)(2,1)} async-done(((bf16[256,32768]{1,0:T(8,128)(2,1)}), bf16[512,32768]{1,0:T(8,128)(2,1)}) %all-gather.5.cloned.1.call-update) | async-done | bytes 33554448 | tf_op jit(solution)/shard_map/all_gather | solution.py:37
  905.0 34.8 %multiply_reduce_fusion = (f32[256]{0:T(256)S(1)}, f32[256,32768]{1,0:T(8,128)}) fusion(f32[256,32768]{1,0:T(8,128)} %convolution_add_fusion, bf16[512,256]{1,0:T(8,128)(2,1)S(1)} %fusion.3, bf16[512,32768]{1,0:T(8,128)(2,1)} %all-gather.5.cloned.1.call-done), kind=kOutput, calls=%fused_computation.5 | convolution fusion | flops 8615100416 | bytes 100926464 | tf_op jit(solution)/shard_map/dot_general | solution.py:35
  939.8 32.9 %psum.31 = f32[256]{0:T(256)S(1)} all-reduce(f32[256]{0:T(256)S(1)} %get-tuple-element.7), channel_id=1, replica_groups=mesh['player'=2,'feat'=16] {'feat'}, use_global_device_ids=true, to_apply=%region_5.6 | all-reduce | flops 256 | bytes 2048 | tf_op jit(solution)/shard_map/psum | solution.py:43
  972.7 17.5 %multiply_convert_fusion = bf16[256,32768]{1,0:T(8,128)(2,1)} fusion(f32[256,32768]{1,0:T(8,128)} %get-tuple-element.8, f32[256]{0:T(256)S(1)} %divide_sqrt_fusion), kind=kLoop, calls=%fused_computation.4 | loop fusion | flops 16777216 | bytes 50332672 | tf_op jit(solution)/shard_map/convert_element_type | solution.py:44
  (5 shorter events, 0.0 us)
Async XLA Ops:
  7.4 104.3 %all-reduce.3.cloned.1.call-start = ((), (), s32[]{:S(2)}) async-start(), calls=%async_computation | async-start | bytes 262144 | tf_op jit(solution)/shard_map/psum | solution.py:22
  20.7 396.0 %all-gather.3.cloned.1.call-start = ((), (), s32[]{:S(2)}) async-start(), calls=%async_computation.1 | async-start | bytes 50331648 | tf_op jit(solution)/shard_map/all_gather | solution.py:37
  21.3 578.9 %all-reduce.5.cloned.1.call-start = ((), (), s32[]{:S(2)}) async-start(), calls=%async_computation.2 | async-start | bytes 262144 | tf_op jit(solution)/shard_map/psum | solution.py:22
  515.4 389.6 %all-gather.5.cloned.1.call-start = ((), (), s32[]{:S(2)}) async-start(), calls=%async_computation.3 | async-start | bytes 50331648 | tf_op jit(solution)/shard_map/all_gather | solution.py:37
Sparse Core Ops, SparseCore 0:
  20.8 90.8 all-reduce.2
  515.5 84.5 all-reduce.4
Sparse Core Ops, SparseCore 1:
  22.7 393.9 all-gather.2
  517.4 387.5 all-gather.4
where the time goes:
time: 998 us
  waiting for transfers between devices  715 us (72%)
  matrix products  147 us (15%)
  blocking collectives  86 us (9%)
  other arithmetic  35 us (4%)
  between operations  14.9 us (1%)
    all_gather x2, waiting for transfers between devices, on_device(): lax.all_gather(weights, 'player', axis=0, tiled=True)  539 us
    psum x2, waiting for transfers between devices, on_device(): proj_own = lax.psum(partial_proj, 'feat')  175 us
    dot_general x2, matrix products, on_device(): lax.dot_general(coeff, lax.all_gather(weights, 'player', axis=0, tiled=Tr...  69.6 us
    psum x2, blocking collectives, on_device(): total = lax.psum(squares, 'feat')  66.1 us
    dot_general x2, matrix products, on_device(): reward = jnp.dot(scaled, slab, preferred_element_type=jnp.float32)  47.6 us
    convert_element_type x2, other arithmetic, on_device(): (update * jnp.sqrt(F / (total + 1e-06))[:, None]).astype(jnp.bfloat16)  34.9 us
    dot_general x2, matrix products, on_device(): lax.dot_general(weights, slab, (((1,), (1,)), ((), ())), preferred_elemen...  26.6 us
    all_gather x2, blocking collectives, on_device(): proj_all = lax.all_gather(proj_own, 'player', axis=0, tiled=True)  20 us
  transfers between devices with their start and end apart: 4, of which 4 were waited for; matrix products, arithmetic and copies ran while one was open for 5% of the time, Pallas kernels for 0%

commit v1 on v0

v1 whole, which is shorter than its diff:
```python
import functools

import jax
import jax.numpy as jnp
from jax import lax
from jax.experimental import pallas as pl
from jax.experimental.pallas import tpu as pltpu
from jax.sharding import PartitionSpec as P


EARLY = (1, 3, 4, 8)
LATE = (2, 2, 4, 4, 2, 1, 1)
UNIT = 32
BLOCK = 1024


HIGH = lax.Precision.HIGHEST


def dot(a, b, contract=((1,), (0,)), precision=None):
    return lax.dot_general(
        a, b, (contract, ((), ())), precision=precision, preferred_element_type=jnp.float32
    )


def through_bf16(x):
    return x.astype(jnp.bfloat16).astype(jnp.float32)


def scatter_sum(x, axis):
    size = lax.axis_size(axis)
    me = lax.axis_index(axis)
    step = 1
    while step < size:
        half = x.shape[0] // 2
        low, high = x[:half], x[half:]
        upper = (me & step) != 0
        send = jnp.where(upper, low, high)
        keep = jnp.where(upper, high, low)
        got = lax.ppermute(send, axis, [(i, i ^ step) for i in range(size)])
        x = keep + got
        step = step * 2
    return x


def gather_back(x, axis):
    size = lax.axis_size(axis)
    me = lax.axis_index(axis)
    step = size // 2
    while step:
        got = lax.ppermute(x, axis, [(i, i ^ step) for i in range(size)])
        upper = (me & step) != 0
        x = jnp.concatenate([jnp.where(upper, got, x), jnp.where(upper, x, got)], axis=-2)
        step = step // 2
    return x


def coeff_kernel(rows, features, gram_ref, down_ref, across_ref, j0_ref, j1_ref, d0_ref, d1_ref):
    span = j0_ref.shape[0]
    batch = gram_ref.shape[0] - span
    rest = span - rows
    inverse_square = 1.0 / features / features
    rhs = ((1,), (1,))

    def coefficients(left, right, first):
        corr = dot(left, right, rhs, HIGH) * inverse_square
        down, across = down_ref[first:, :], across_ref[...]
        mixing = jnp.where(across < down, -through_bf16(corr), 0.0)
        mixing = jnp.where(across == down, 1.0, mixing)
        return through_bf16(left / features), mixing

    def scale(left, product):
        norm = jnp.maximum(jnp.sum(left * product, axis=1, keepdims=True), 0.0)
        return jnp.sqrt(features / (norm + 1e-06))

    proj = gram_ref[batch:, :batch]
    reward, mixing = coefficients(proj, proj, 0)
    j0 = jnp.concatenate([reward, mixing], axis=1)
    y0 = dot(j0, gram_ref[...], precision=HIGH)
    d0 = scale(j0, y0)
    j0_ref[...] = j0.astype(jnp.bfloat16)
    d0_ref[...] = d0
    proj1 = d0 * y0[:, :batch]
    reward, mixing = coefficients(proj1[rest:], proj1, rest)
    j1_ref[:, :batch] = reward.astype(jnp.bfloat16)
    j1_ref[:, batch:] = mixing.astype(jnp.bfloat16)
    joint = dot(mixing, d0 * j0, precision=HIGH)
    joint = jnp.concatenate([joint[:, :batch] + reward, joint[:, batch:]], axis=1)
    d1_ref[...] = scale(joint, dot(joint, gram_ref[...], precision=HIGH))


def coefficients_of(gram, order, rows, features):
    span = order.shape[0]
    size = gram.shape[0]
    return pl.pallas_call(
        functools.partial(coeff_kernel, rows, features),
        out_shape=[
            jax.ShapeDtypeStruct((span, size), jnp.bfloat16),
            jax.ShapeDtypeStruct((rows, size), jnp.bfloat16),
            jax.ShapeDtypeStruct((span, 1), jnp.float32),
            jax.ShapeDtypeStruct((rows, 1), jnp.float32),
        ],
        cost_estimate=pl.CostEstimate(
            flops=24 * size * size * span, bytes_accessed=8 * size * size, transcendentals=0
        ),
        name="coefficients_of",
    )(gram, order[:, None], order[None, :])


def update_kernel(others, base_ref, w_ref, x_ref, *refs):
    other_refs = refs[:others]
    j0_ref, j1_ref, d0_ref, d1_ref = refs[others : others + 4]
    out_ref, stack, scaled = refs[-3:]
    rows, batch = w_ref.shape[0], x_ref.shape[0]
    rest = others * rows
    split = batch + rest
    stack[:batch, :] = x_ref[...]
    scaled[:batch, :] = x_ref[...]
    for i in range(others):
        stack[batch + i * rows : batch + (i + 1) * rows, :] = other_refs[i][...]
    stack[split:, :] = w_ref[...]
    first = dot(j0_ref[:rest, :split], stack[:split, :])
    scaled[batch:split, :] = (first * d0_ref[:rest, :]).astype(jnp.bfloat16)
    own = dot(j0_ref[rest:, :], stack[...])
    scaled[split:, :] = (own * d0_ref[rest:, :]).astype(jnp.bfloat16)
    out_ref[...] = (dot(j1_ref[...], scaled[...]) * d1_ref[...]).astype(jnp.bfloat16)


def update_piece(base, weights, slab, others, coeffs, out, width, block):
    rows, batch = weights.shape[0], slab.shape[0]
    count = len(others)
    shift = lambda i, b: (0, b[0] + i)
    whole = lambda i, b: (0, 0)
    in_specs = [pl.BlockSpec((rows, block), shift), pl.BlockSpec((batch, block), shift)]
    in_specs += [pl.BlockSpec((rows, block), lambda i, b: (0, i))] * count
    in_specs += [pl.BlockSpec(c.shape, whole) for c in coeffs]
    operands = [weights, slab, *others, *coeffs]
    aliases = {}
    if out is not None:
        in_specs.append(pl.BlockSpec(memory_space=pl.ANY))
        operands.append(out)
        aliases = {len(operands): 0}
    total = rows * (count + 1)
    return pl.pallas_call(
        functools.partial(update_kernel, count),
        out_shape=jax.ShapeDtypeStruct(weights.shape, jnp.bfloat16),
        grid_spec=pltpu.PrefetchScalarGridSpec(
            num_scalar_prefetch=1,
            grid=(width // block,),
            in_specs=in_specs,
            out_specs=pl.BlockSpec((rows, block), shift),
            scratch_shapes=[
                pltpu.VMEM((total + batch, block), jnp.bfloat16),
                pltpu.VMEM((total + batch, block), jnp.bfloat16),
            ],
        ),
        input_output_aliases=aliases,
        compiler_params=pltpu.CompilerParams(dimension_semantics=("arbitrary",)),
        cost_estimate=pl.CostEstimate(
            flops=2 * width * (total + batch) * (total + rows),
            bytes_accessed=2 * width * (2 * rows + batch + count * rows),
            transcendentals=0,
        ),
        name="update_piece",
    )(base, *operands)


def compute(slab, players):
    rows, width = players.shape
    batch = slab.shape[0]
    n = lax.axis_size("player")
    me = lax.axis_index("player")
    features = width * lax.axis_size("feat")
    half, unit = width // 2, width // UNIT
    ring = [[(i, (i + s) % n) for i in range(n)] for s in range(n)]

    sent_at = [jnp.where(me + s < n, 0, half) for s in range(n)]
    got_at = [jnp.where(me - s >= 0, 0, half) for s in range(n)]

    def send(s, start, size):
        piece = lax.dynamic_slice(players, (0, start), (rows, size))
        return lax.ppermute(piece, "player", ring[s])

    early, late, place = [], [], 0
    for units in EARLY:
        size = units * unit
        early.append((place, size, [send(s, sent_at[s] + place, size) for s in range(1, n)]))
        place += size
    place = 0
    for units in LATE:
        size = units * unit
        late.append(
            (
                place,
                size,
                [send(s, half - sent_at[s] + place, size) for s in range(1, n)],
            )
        )
        place += size

    rhs = ((1,), (1,))
    own_gram = dot(players, players, rhs)
    own_proj = dot(players, slab, rhs)
    slab_gram = dot(slab, slab, rhs)
    cross = []
    for s in range(1, n):
        total = 0.0
        for place, size, got in early:
            mine = lax.dynamic_slice(players, (0, got_at[s] + place), (rows, size))
            total = total + dot(mine, got[s - 1], rhs)
        cross.append(total)

    if batch >= rows:
        flat = [slab_gram[i : i + rows] for i in range(0, batch, rows)]
    else:
        flat = [jnp.pad(slab_gram, ((0, rows - batch), (0, 0)))]
    payload = jnp.concatenate([own_gram, *cross, own_proj, *flat], axis=1)
    part = scatter_sum(payload, "feat")
    parts = [part] + [lax.ppermute(part, "player", ring[s]) for s in range(1, n)]
    full = gather_back(jnp.stack(parts), "feat")

    span = n * rows
    turn = [*range(1, n), 0]
    block_of = lambda t, u: full[t, :, ((u - t) % n) * rows : ((u - t) % n + 1) * rows]
    pair = lambda t, u: block_of(t, u) if t == u else block_of(t, u) + block_of(u, t).T
    proj = jnp.concatenate([full[t, :, span : span + batch] for t in turn], axis=0)
    tail = full[0, :, span + batch :]
    if batch >= rows:
        hmat = jnp.concatenate(
            [tail[:, i * batch : (i + 1) * batch] for i in range(batch // rows)], axis=0
        )
    else:
        hmat = tail[:batch]
    lines = [jnp.concatenate([hmat, proj.T], axis=1)]
    for k, t in enumerate(turn):
        left = proj[k * rows : (k + 1) * rows]
        lines.append(jnp.concatenate([left, *[pair(t, u) for u in turn]], axis=1))
    gram = jnp.concatenate(lines, axis=0)
    order = jnp.concatenate(
        [((me - t) % n) * rows + jnp.arange(rows, dtype=jnp.int32) for t in turn]
    )
    coeffs = coefficients_of(gram, order, rows, features)

    block = min(BLOCK, unit)
    first = jnp.where(me > 0, 0, half)
    out = None
    for start, pieces in ((first, early), (half - first, late)):
        for place, size, got in pieces:
            base = ((start + place) // block).reshape(1).astype(jnp.int32)
            out = update_piece(base, players, slab, got, coeffs, out, size, block)
    return out


def solution(mesh):
    in_specs = (P(None, "feat"), P("player", "feat"))
    out_specs = P("player", "feat")
    return jax.shard_map(
        compute, mesh=mesh, in_specs=in_specs, out_specs=out_specs, check_vma=False
    )
```

time: 998 us -> 438 us (0.44)
  waiting for transfers between devices: 715 us -> 249 us
  matrix products: 147 us -> 44.3 us
  blocking collectives: 86 us -> 0 us
  Pallas kernels: 0 us -> 82.3 us
  starting transfers between devices: 0.13 us -> 28 us
  other arithmetic: 35 us -> 8.31 us
  local copies, waits for them, and re-layouts: 0 us -> 25.1 us
  between operations: 14.9 us -> 0.35 us
    all_gather x2 -> x0, waiting for transfers between devices: 539 us -> none  [on_device(): lax.all_gather(weights, 'player', axis=0, tiled=True)]
    ppermute x0 -> x20, waiting for transfers between devices: none -> 249 us  [the longest x11 221 us: send(): return lax.ppermute(piece, 'player', ring[s])]
    psum x2 -> x0, waiting for transfers between devices: 175 us -> none  [on_device(): proj_own = lax.psum(partial_proj, 'feat')]
    dot_general x8 -> x7, matrix products: 147 us -> 44.3 us  [dot(): lax.dot_general(a, b, (contract, ((), ())), precision=precision, preferre...]
    pallas_call x0 -> x12, Pallas kernels: none -> 82.3 us  [the longest x11 70.5 us: update_piece(): pl.pallas_call(functools.partial(update_kernel, count), out_shape=jax.Sha...]
    psum x2 -> x0, blocking collectives: 66.1 us -> none  [on_device(): total = lax.psum(squares, 'feat')]
    convert_element_type x2 -> x0, other arithmetic: 34.9 us -> none  [on_device(): (update * jnp.sqrt(F / (total + 1e-06))[:, None]).astype(jnp.bfloat16)]
    ppermute x0 -> x20, starting transfers between devices: none -> 28 us  [the longest x11 12.7 us: send(): return lax.ppermute(piece, 'player', ring[s])]
  transfers between devices with their start and end apart: 4 -> 20, of which waited for: 4 -> 14; matrix products, arithmetic and copies ran while one was open for 5% -> 15% of each run, Pallas kernels for 0% -> 18%
where the time goes in v1:
time: 438 us; the launch traced here: 437 us
  waiting for transfers between devices  249 us (57%)
  Pallas kernels  82.3 us (19%)
  matrix products  44.3 us (10%)
  starting transfers between devices  28 us (6%)
  local copies, waits for them, and re-layouts  25.1 us (6%)
  other arithmetic  8.31 us (2%)
    ppermute x11, waiting for transfers between devices, send(): return lax.ppermute(piece, 'player', ring[s])  221 us
    pallas_call x11, Pallas kernels, update_piece(): pl.pallas_call(functools.partial(update_kernel, count), out_shape=jax.Sha...  70.5 us
    dot_general x7, matrix products, dot(): lax.dot_general(a, b, (contract, ((), ())), precision=precision, preferre...  44.3 us
    dynamic_slice x5, local copies, waits for them, and re-layouts, send(): piece = lax.dynamic_slice(players, (0, start), (rows, size))  19.4 us
    ppermute x4, waiting for transfers between devices, gather_back(): got = lax.ppermute(x, axis, [(i, i ^ step) for i in range(size)])  13 us
    ppermute x11, starting transfers between devices, send(): return lax.ppermute(piece, 'player', ring[s])  12.7 us
    ppermute x4, waiting for transfers between devices, scatter_sum(): got = lax.ppermute(send, axis, [(i, i ^ step) for i in range(size)])  12.1 us
    pallas_call x1, Pallas kernels, coefficients_of(): pl.pallas_call(functools.partial(coeff_kernel, rows, features), out_shape...  11.8 us
  transfers between devices with their start and end apart: 20, of which 14 were waited for; matrix products, arithmetic and copies ran while one was open for 15% of the time, Pallas kernels for 18%

profile of v1, /device:TPU:0, one launch (start us, length us, event | category | flops | bytes accessed | tf_op | source)
XLA Modules:
  0.0 436.9 jit_solution(7848897392985390291)
XLA Ops:
  0.0 5.8 %constant_dynamic-slice_fusion.2 = (bf16[256,4096]{1,0:T(8,128)(2,1)}, bf16[256,4096]{1,0:T(8,128)(2,1)}, bf16[256,4096]{1,0:T(8,128)(2,1)}) fusion(bf16[256,32768]{1,0:T(8,128)(2,1)} %w_ref.21, s32[]{:T(128)S(6)} %select_n.237, s32[]{:T(128)S(6)} %select_n.235, s32[]{:T(128)S(6)} %select_n.209), kind=kLoop, calls=%fused_computation.47 | loop fusion | bytes 12582924 | tf_op jit(solution)/shard_map/dynamic_slice | solution.py:181
  11.3 4.6 %constant_dynamic-slice_fusion.6 = bf16[256,8192]{1,0:T(8,128)(2,1)} fusion(bf16[256,32768]{1,0:T(8,128)(2,1)} %w_ref.21, s32[]{:T(128)S(6)} %select_n.211), kind=kLoop, calls=%fused_computation.51 | loop fusion | bytes 8388612 | tf_op jit(solution)/shard_map/dynamic_slice | solution.py:181
  20.7 13.6 %fusion.14 = f32[256,256]{1,0:T(8,128)} fusion(bf16[256,32768]{1,0:T(8,128)(2,1)} %w_ref.21), kind=kOutput, calls=%fused_computation.63 | convolution fusion | flops 4294967296 | bytes 17039360 | tf_op jit(solution)/shard_map/dot_general | solution.py:21
  34.3 8.1 %fusion.16 = f32[128,128]{1,0:T(8,128)S(1)} fusion(bf16[128,32768]{1,0:T(8,128)(2,1)} %x_ref.21), kind=kOutput, calls=%fused_computation.65 | convolution fusion | flops 1073741824 | bytes 8454144 | tf_op jit(solution)/shard_map/dot_general | solution.py:21
  42.4 10.7 %fusion.15 = f32[256,128]{1,0:T(8,128)S(1)} fusion(bf16[256,32768]{1,0:T(8,128)(2,1)} %w_ref.21, bf16[128,32768]{1,0:T(8,128)(2,1)} %x_ref.21), kind=kOutput, calls=%fused_computation.64 | convolution fusion | flops 2147483648 | bytes 25296896 | tf_op jit(solution)/shard_map/dot_general | solution.py:21
  53.1 136.4 %collective-permute-done.2.refs_0_ = bf16[256,3072]{1,0:T(8,128)(2,1)} collective-permute-done((bf16[256,3072]{1,0:T(8,128)(2,1)}, bf16[256,3072]{1,0:T(8,128)(2,1)}, u32[]{:S(2)}, u32[]{:S(2)}) %collective-permute-start.2) | collective-permute-done | bytes 1572896 | tf_op jit(solution)/shard_map/ppermute | solution.py:182
  195.2 4.8 %fusion = f32[256,256]{1,0:T(8,128)S(1)} fusion(bf16[256,8192]{1,0:T(8,128)(2,1)} %collective-permute-done.4.refs_0_, bf16[256,32768]{1,0:T(8,128)(2,1)} %w_ref.21, s32[]{:T(128)S(6)} %select_n.210), kind=kOutput, calls=%fused_computation | convolution fusion | flops 1073741824 | bytes 8650756 | tf_op jit(solution)/shard_map/dot_general | solution.py:21
  206.3 5.2 %collective-permute-done.6 = f32[64,768]{1,0:T(8,128)S(1)} collective-permute-done((f32[64,768]{1,0:T(8,128)S(1)}, f32[64,768]{1,0:T(8,128)S(1)}, u32[]{:S(2)}, u32[]{:S(2)}) %collective-permute-start.6) | collective-permute-done | bytes 196640 | tf_op jit(solution)/shard_map/ppermute | solution.py:40
  239.2 6.2 %collective-permute-done.12 = f32[2,64,768]{2,1,0:T(8,128)S(1)} collective-permute-done((f32[2,64,768]{2,1,0:T(8,128)S(1)}, f32[2,64,768]{2,1,0:T(8,128)S(1)}, u32[]{:S(2)}, u32[]{:S(2)}) %collective-permute-start.12) | collective-permute-done | bytes 393248 | tf_op jit(solution)/shard_map/ppermute | solution.py:51
  266.1 11.8 %coefficients_of.1 = (bf16[512,640]{1,0:T(8,128)(2,1)}, bf16[256,640]{1,0:T(8,128)(2,1)}, f32[512,1]{1,0:T(8,128)}, f32[256,1]{1,0:T(8,128)}) custom-call(f32[640,640]{1,0:T(8,128)} %maximum_maximum_fusion.gram_ref, s32[512,1]{1,0:T(8,128)} %copy.39.down_ref, s32[1,512]{1,0:T(1,128)} %bitcast.55), custom_call_target="tpu_custom_call" | custom-call | flops 5033164800 | bytes 3276800 | tf_op jit(solution)/shard_map/coefficients_of/pallas_call | solution.py:95
  281.7 6.6 %update_piece.12.refs_5_ = bf16[256,32768]{1,0:T(8,128)(2,1)} custom-call(s32[1]{0:T(128)} %bitcast.23.base_ref, bf16[256,32768]{1,0:T(8,128)(2,1)} %w_ref.21, bf16[128,32768]{1,0:T(8,128)(2,1)} %x_ref.21, bf16[256,3072]{1,0:T(8,128)(2,1)} %collective-permute-done.2.refs_0_, ...), custom_call_target="tpu_custom_call", output_to_operand_aliasing={{}: (8, {})} | custom-call | flops 3019898880 | bytes 5505024 | tf_op jit(solution)/shard_map/update_piece/pallas_call | solution.py:144
  288.2 8.0 %update_piece.13.refs_5_ = bf16[256,32768]{1,0:T(8,128)(2,1)} custom-call(s32[1]{0:T(128)} %bitcast.22.base_ref, bf16[256,32768]{1,0:T(8,128)(2,1)} %w_ref.21, bf16[128,32768]{1,0:T(8,128)(2,1)} %x_ref.21, bf16[256,4096]{1,0:T(8,128)(2,1)} %copy-done, bf16[512,640]{1,0:T(8,128)(2,1)} %get-tuple-element.9.refs_1_, ...), custom_call_target="tpu_custom_call", output_to_operand_aliasing={{}: (8, {})} | custom-call | flops 4026531840 | bytes 7340032 | tf_op jit(solution)/shard_map/update_piece/pallas_call | solution.py:144
  296.2 13.5 %update_piece.14.refs_5_ = bf16[256,32768]{1,0:T(8,128)(2,1)} custom-call(s32[1]{0:T(128)} %bitcast.21.base_ref, bf16[256,32768]{1,0:T(8,128)(2,1)} %w_ref.21, bf16[128,32768]{1,0:T(8,128)(2,1)} %x_ref.21, bf16[256,8192]{1,0:T(8,128)(2,1)} %collective-permute-done.4.refs_0_, ...), custom_call_target="tpu_custom_call", output_to_operand_aliasing={{}: (8, {})} | custom-call | flops 8053063680 | bytes 14680064 | tf_op jit(solution)/shard_map/update_piece/pallas_call | solution.py:144
  310.3 5.2 %update_piece.15.refs_5_ = bf16[256,32768]{1,0:T(8,128)(2,1)} custom-call(s32[1]{0:T(128)} %bitcast.20.base_ref, bf16[256,32768]{1,0:T(8,128)(2,1)} %w_ref.21, bf16[128,32768]{1,0:T(8,128)(2,1)} %x_ref.21, bf16[256,2048]{1,0:T(8,128)(2,1)} %collective-permute-done.19.refs_0_, ...), custom_call_target="tpu_custom_call", output_to_operand_aliasing={{}: (8, {})} | custom-call | flops 2013265920 | bytes 3670016 | tf_op jit(solution)/shard_map/update_piece/pallas_call | solution.py:144
  317.1 5.1 %update_piece.16.refs_5_ = bf16[256,32768]{1,0:T(8,128)(2,1)} custom-call(s32[1]{0:T(128)} %bitcast.19.base_ref, bf16[256,32768]{1,0:T(8,128)(2,1)} %w_ref.21, bf16[128,32768]{1,0:T(8,128)(2,1)} %x_ref.21, bf16[256,2048]{1,0:T(8,128)(2,1)} %copy-done.2, bf16[512,640]{1,0:T(8,128)(2,1)} %get-tuple-element.9.refs_1_, ...), custom_call_target="tpu_custom_call", output_to_operand_aliasing={{}: (8, {})} | custom-call | flops 2013265920 | bytes 3670016 | tf_op jit(solution)/shard_map/update_piece/pallas_call | solution.py:144
  322.2 20.8 %collective-permute-done.17.refs_0_ = bf16[256,4096]{1,0:T(8,128)(2,1)} collective-permute-done((bf16[256,4096]{1,0:T(8,128)(2,1)}, bf16[256,4096]{1,0:T(8,128)(2,1)}, u32[]{:S(2)}, u32[]{:S(2)}) %collective-permute-start.17) | collective-permute-done | bytes 2097184 | tf_op jit(solution)/shard_map/ppermute | solution.py:182
  343.0 7.9 %update_piece.17.refs_5_ = bf16[256,32768]{1,0:T(8,128)(2,1)} custom-call(s32[1]{0:T(128)} %bitcast.18.base_ref, bf16[256,32768]{1,0:T(8,128)(2,1)} %w_ref.21, bf16[128,32768]{1,0:T(8,128)(2,1)} %x_ref.21, bf16[256,4096]{1,0:T(8,128)(2,1)} %collective-permute-done.17.refs_0_, ...), custom_call_target="tpu_custom_call", output_to_operand_aliasing={{}: (8, {})} | custom-call | flops 4026531840 | bytes 7340032 | tf_op jit(solution)/shard_map/update_piece/pallas_call | solution.py:144
  350.9 37.0 %collective-permute-done.16.refs_0_ = bf16[256,4096]{1,0:T(8,128)(2,1)} collective-permute-done((bf16[256,4096]{1,0:T(8,128)(2,1)}, bf16[256,4096]{1,0:T(8,128)(2,1)}, u32[]{:S(2)}, u32[]{:S(2)}) %collective-permute-start.16) | collective-permute-done | bytes 2097184 | tf_op jit(solution)/shard_map/ppermute | solution.py:182
  388.0 7.9 %update_piece.18.refs_5_ = bf16[256,32768]{1,0:T(8,128)(2,1)} custom-call(s32[1]{0:T(128)} %bitcast.17.base_ref, bf16[256,32768]{1,0:T(8,128)(2,1)} %w_ref.21, bf16[128,32768]{1,0:T(8,128)(2,1)} %x_ref.21, bf16[256,4096]{1,0:T(8,128)(2,1)} %collective-permute-done.16.refs_0_, ...), custom_call_target="tpu_custom_call", output_to_operand_aliasing={{}: (8, {})} | custom-call | flops 4026531840 | bytes 7340032 | tf_op jit(solution)/shard_map/update_piece/pallas_call | solution.py:144
  395.9 14.6 %collective-permute-done.15.refs_0_ = bf16[256,2048]{1,0:T(8,128)(2,1)} collective-permute-done((bf16[256,2048]{1,0:T(8,128)(2,1)}, bf16[256,2048]{1,0:T(8,128)(2,1)}, u32[]{:S(2)}, u32[]{:S(2)}) %collective-permute-start.15) | collective-permute-done | bytes 1048608 | tf_op jit(solution)/shard_map/ppermute | solution.py:182
  410.5 5.1 %update_piece.19.refs_5_ = bf16[256,32768]{1,0:T(8,128)(2,1)} custom-call(s32[1]{0:T(128)} %bitcast.16.base_ref, bf16[256,32768]{1,0:T(8,128)(2,1)} %w_ref.21, bf16[128,32768]{1,0:T(8,128)(2,1)} %x_ref.21, bf16[256,2048]{1,0:T(8,128)(2,1)} %collective-permute-done.15.refs_0_, ...), custom_call_target="tpu_custom_call", output_to_operand_aliasing={{}: (8, {})} | custom-call | flops 2013265920 | bytes 3670016 | tf_op jit(solution)/shard_map/update_piece/pallas_call | solution.py:144
  415.6 6.0 %collective-permute-done.14.refs_0_ = bf16[256,1024]{1,0:T(8,128)(2,1)S(1)} collective-permute-done((bf16[256,1024]{1,0:T(8,128)(2,1)S(1)}, bf16[256,1024]{1,0:T(8,128)(2,1)S(1)}, u32[]{:S(2)}, u32[]{:S(2)}) %collective-permute-start.14) | collective-permute-done | bytes 524320 | tf_op jit(solution)/shard_map/ppermute | solution.py:182
  422.4 3.7 update_piece.20.refs_5_
  426.1 6.2 %collective-permute-done.refs_0_ = bf16[256,1024]{1,0:T(8,128)(2,1)S(1)} collective-permute-done((bf16[256,1024]{1,0:T(8,128)(2,1)S(1)}, bf16[256,1024]{1,0:T(8,128)(2,1)S(1)}, u32[]{:S(2)}, u32[]{:S(2)}) %collective-permute-start) | collective-permute-done | bytes 524320 | tf_op jit(solution)/shard_map/ppermute | solution.py:182
  (91 shorter events, 81.6 us)
Async XLA Ops:
  5.8 186.2 %collective-permute-start.3 = (bf16[256,4096]{1,0:T(8,128)(2,1)}, bf16[256,4096]{1,0:T(8,128)(2,1)S(1)}, u32[]{:S(2)}, u32[]{:S(2)}) collective-permute-start(bf16[256,4096]{1,0:T(8,128)(2,1)} %get-tuple-element.20), channel_id=1, source_target_pairs={{0,16},{16,0},{1,17},{17,1},{2,18},{18,2},{3,19},{19,3},{4,20},{20... | collective-permute-start | bytes 6291464 | tf_op jit(solution)/shard_map/ppermute | solution.py:182
  11.3 188.6 %collective-permute-start.1 = (bf16[256,1024]{1,0:T(8,128)(2,1)}, bf16[256,1024]{1,0:T(8,128)(2,1)S(1)}, u32[]{:S(2)}, u32[]{:S(2)}) collective-permute-start(bf16[256,1024]{1,0:T(8,128)(2,1)} %get-tuple-element.22), channel_id=1, source_target_pairs={{0,16},{16,0},{1,17},{17,1},{2,18},{18,2},{3,19},{19,3},{4,20},{20... | collective-permute-start | bytes 1572872 | tf_op jit(solution)/shard_map/ppermute | solution.py:182
  16.0 179.2 %collective-permute-start.4 = (bf16[256,8192]{1,0:T(8,128)(2,1)}, bf16[256,8192]{1,0:T(8,128)(2,1)}, u32[]{:S(2)}, u32[]{:S(2)}) collective-permute-start(bf16[256,8192]{1,0:T(8,128)(2,1)} %constant_dynamic-slice_fusion.6), channel_id=1, source_target_pairs={{0,16},{16,0},{1,17},{17,1},{2,18},{18,2},{3,19},{19,3},{4,20},{20... | collective-permute-start | bytes 12582920 | tf_op jit(solution)/shard_map/ppermute | solution.py:182
  20.7 168.8 %collective-permute-start.2 = (bf16[256,3072]{1,0:T(8,128)(2,1)}, bf16[256,3072]{1,0:T(8,128)(2,1)}, u32[]{:S(2)}, u32[]{:S(2)}) collective-permute-start(bf16[256,3072]{1,0:T(8,128)(2,1)} %constant_dynamic-slice_fusion.8), channel_id=1, source_target_pairs={{0,16},{16,0},{1,17},{17,1},{2,18},{18,2},{3,19},{19,3},{4,20},{20... | collective-permute-start | bytes 4718600 | tf_op jit(solution)/shard_map/ppermute | solution.py:182
  192.0 9.6 %copy-start = (bf16[256,4096]{1,0:T(8,128)(2,1)}, bf16[256,4096]{1,0:T(8,128)(2,1)S(1)}, u32[]{:S(2)}) copy-start(bf16[256,4096]{1,0:T(8,128)(2,1)S(1)} %collective-permute-done.3.refs_0_) | copy-start | bytes 6291460
  199.9 49.3 %copy-start.1 = (bf16[256,1024]{1,0:T(8,128)(2,1)}, bf16[256,1024]{1,0:T(8,128)(2,1)S(1)}, u32[]{:S(2)}) copy-start(bf16[256,1024]{1,0:T(8,128)(2,1)S(1)} %collective-permute-done.1.refs_0_) | copy-start | bytes 1572868
  202.4 1.9 collective-permute-start.5
  204.4 7.0 %collective-permute-start.6 = (f32[64,768]{1,0:T(8,128)S(1)}, f32[64,768]{1,0:T(8,128)S(1)}, u32[]{:S(2)}, u32[]{:S(2)}) collective-permute-start(f32[64,768]{1,0:T(8,128)S(1)} %slice_select_fusion.1), channel_id=1, source_target_pairs={{0,2},{1,3},{2,0},{3,1},{4,6},{5,7},{6,4},{7,5},{8,10},{9,11},{10,... | collective-permute-start | bytes 589832 | tf_op jit(solution)/shard_map/ppermute | solution.py:40
  211.5 4.7 %collective-permute-start.7 = (f32[32,768]{1,0:T(8,128)S(1)}, f32[32,768]{1,0:T(8,128)S(1)}, u32[]{:S(2)}, u32[]{:S(2)}) collective-permute-start(f32[32,768]{1,0:T(8,128)S(1)} %slice_select_fusion.2), channel_id=1, source_target_pairs={{0,4},{1,5},{2,6},{3,7},{4,0},{5,1},{6,2},{7,3},{8,12},{9,13},{10,... | collective-permute-start | bytes 294920 | tf_op jit(solution)/shard_map/ppermute | solution.py:40
  216.2 5.1 %collective-permute-start.8 = (f32[16,768]{1,0:T(8,128)S(1)}, f32[16,768]{1,0:T(8,128)S(1)}, u32[]{:S(2)}, u32[]{:S(2)}) collective-permute-start(f32[16,768]{1,0:T(8,128)S(1)} %slice_select_fusion.3), channel_id=1, source_target_pairs={{0,8},{1,9},{2,10},{3,11},{4,12},{5,13},{6,14},{7,15},{8,0},{9,1},... | collective-permute-start | bytes 147464 | tf_op jit(solution)/shard_map/ppermute | solution.py:40
  221.3 4.2 collective-permute-start.9
  225.5 6.0 %collective-permute-start.10 = (f32[2,16,768]{2,1,0:T(8,128)S(1)}, f32[2,16,768]{2,1,0:T(8,128)S(1)}, u32[]{:S(2)}, u32[]{:S(2)}) collective-permute-start(f32[2,16,768]{2,1,0:T(8,128)S(1)} %pad_maximum_fusion.10), channel_id=1, source_target_pairs={{0,8},{1,9},{2,10},{3,11},{4,12},{5,13},{6,14},{7,15},{8,0},{9,1},... | collective-permute-start | bytes 294920 | tf_op jit(solution)/shard_map/ppermute | solution.py:51
  231.5 6.0 %collective-permute-start.11 = (f32[2,32,768]{2,1,0:T(8,128)S(1)}, f32[2,32,768]{2,1,0:T(8,128)S(1)}, u32[]{:S(2)}, u32[]{:S(2)}) collective-permute-start(f32[2,32,768]{2,1,0:T(8,128)S(1)} %pad_maximum_fusion.7), channel_id=1, source_target_pairs={{0,4},{1,5},{2,6},{3,7},{4,0},{5,1},{6,2},{7,3},{8,12},{9,13},{10,... | collective-permute-start | bytes 589832 | tf_op jit(solution)/shard_map/ppermute | solution.py:51
  237.6 7.8 %collective-permute-start.12 = (f32[2,64,768]{2,1,0:T(8,128)S(1)}, f32[2,64,768]{2,1,0:T(8,128)S(1)}, u32[]{:S(2)}, u32[]{:S(2)}) collective-permute-start(f32[2,64,768]{2,1,0:T(8,128)S(1)} %pad_maximum_fusion.2), channel_id=1, source_target_pairs={{0,2},{1,3},{2,0},{3,1},{4,6},{5,7},{6,4},{7,5},{8,10},{9,11},{10,... | collective-permute-start | bytes 1179656 | tf_op jit(solution)/shard_map/ppermute | solution.py:51
  245.5 8.7 %collective-permute-start.13 = (f32[2,128,768]{2,1,0:T(8,128)S(1)}, f32[2,128,768]{2,1,0:T(8,128)}, u32[]{:S(2)}, u32[]{:S(2)}) collective-permute-start(f32[2,128,768]{2,1,0:T(8,128)S(1)} %pad_maximum_fusion), channel_id=1, source_target_pairs={{0,1},{1,0},{2,3},{3,2},{4,5},{5,4},{6,7},{7,6},{8,9},{9,8},{10,11... | collective-permute-start | bytes 2359304 | tf_op jit(solution)/shard_map/ppermute | solution.py:51
  249.3 60.4 %collective-permute-start.19 = (bf16[256,2048]{1,0:T(8,128)(2,1)}, bf16[256,2048]{1,0:T(8,128)(2,1)}, u32[]{:S(2)}, u32[]{:S(2)}) collective-permute-start(bf16[256,2048]{1,0:T(8,128)(2,1)} %get-tuple-element.15), channel_id=1, source_target_pairs={{0,16},{16,0},{1,17},{17,1},{2,18},{18,2},{3,19},{19,3},{4,20},{20... | collective-permute-start | bytes 3145736 | tf_op jit(solution)/shard_map/ppermute | solution.py:182
  250.8 64.7 %collective-permute-start.18 = (bf16[256,2048]{1,0:T(8,128)(2,1)}, bf16[256,2048]{1,0:T(8,128)(2,1)S(1)}, u32[]{:S(2)}, u32[]{:S(2)}) collective-permute-start(bf16[256,2048]{1,0:T(8,128)(2,1)} %get-tuple-element.16), channel_id=1, source_target_pairs={{0,16},{16,0},{1,17},{17,1},{2,18},{18,2},{3,19},{19,3},{4,20},{20... | collective-permute-start | bytes 3145736 | tf_op jit(solution)/shard_map/ppermute | solution.py:182
  251.3 91.7 %collective-permute-start.17 = (bf16[256,4096]{1,0:T(8,128)(2,1)}, bf16[256,4096]{1,0:T(8,128)(2,1)}, u32[]{:S(2)}, u32[]{:S(2)}) collective-permute-start(bf16[256,4096]{1,0:T(8,128)(2,1)} %get-tuple-element.18), channel_id=1, source_target_pairs={{0,16},{16,0},{1,17},{17,1},{2,18},{18,2},{3,19},{19,3},{4,20},{20... | collective-permute-start | bytes 6291464 | tf_op jit(solution)/shard_map/ppermute | solution.py:182
  252.8 135.2 %collective-permute-start.16 = (bf16[256,4096]{1,0:T(8,128)(2,1)}, bf16[256,4096]{1,0:T(8,128)(2,1)}, u32[]{:S(2)}, u32[]{:S(2)}) collective-permute-start(bf16[256,4096]{1,0:T(8,128)(2,1)} %get-tuple-element.19), channel_id=1, source_target_pairs={{0,16},{16,0},{1,17},{17,1},{2,18},{18,2},{3,19},{19,3},{4,20},{20... | collective-permute-start | bytes 6291464 | tf_op jit(solution)/shard_map/ppermute | solution.py:182
  253.4 12.8 %copy-start.8 = (s32[512]{0:T(512)}, s32[512]{0:T(512)S(1)}, u32[]{:S(2)}) copy-start(s32[512]{0:T(512)S(1)} %pad_add_fusion) | copy-start | bytes 6148
  254.2 156.2 %collective-permute-start.15 = (bf16[256,2048]{1,0:T(8,128)(2,1)}, bf16[256,2048]{1,0:T(8,128)(2,1)}, u32[]{:S(2)}, u32[]{:S(2)}) collective-permute-start(bf16[256,2048]{1,0:T(8,128)(2,1)} %get-tuple-element.17), channel_id=1, source_target_pairs={{0,16},{16,0},{1,17},{17,1},{2,18},{18,2},{3,19},{19,3},{4,20},{20... | collective-permute-start | bytes 3145736 | tf_op jit(solution)/shard_map/ppermute | solution.py:182
  296.2 13.5 %copy-start.6 = (bf16[256,1024]{1,0:T(8,128)(2,1)S(1)}, bf16[256,1024]{1,0:T(8,128)(2,1)}, u32[]{:S(2)}) copy-start(bf16[256,1024]{1,0:T(8,128)(2,1)} %get-tuple-element.21) | copy-start | bytes 1572868
  309.7 111.9 %collective-permute-start.14 = (bf16[256,1024]{1,0:T(8,128)(2,1)S(1)}, bf16[256,1024]{1,0:T(8,128)(2,1)S(1)}, u32[]{:S(2)}, u32[]{:S(2)}) collective-permute-start(bf16[256,1024]{1,0:T(8,128)(2,1)S(1)} %copy-done.6), channel_id=1, source_target_pairs={{0,16},{16,0},{1,17},{17,1},{2,18},{18,2},{3,19},{19,3},{4,20},{20... | collective-permute-start | bytes 1572872 | tf_op jit(solution)/shard_map/ppermute | solution.py:182
  315.5 116.8 %collective-permute-start = (bf16[256,1024]{1,0:T(8,128)(2,1)S(1)}, bf16[256,1024]{1,0:T(8,128)(2,1)S(1)}, u32[]{:S(2)}, u32[]{:S(2)}) collective-permute-start(bf16[256,1024]{1,0:T(8,128)(2,1)S(1)} %copy-done.5), channel_id=1, source_target_pairs={{0,16},{16,0},{1,17},{17,1},{2,18},{18,2},{3,19},{19,3},{4,20},{20... | collective-permute-start | bytes 1572872 | tf_op jit(solution)/shard_map/ppermute | solution.py:182
  (5 other events, 17.9 us)

commit v2 on v1

--- a/solution.py
+++ b/solution.py
@@ -8,7 +8,7 @@
 from jax.sharding import PartitionSpec as P
 
 
-EARLY = (1, 3, 4, 8)
+EARLY = (1, 3, 8, 4)
 LATE = (2, 2, 4, 4, 2, 1, 1)
 UNIT = 32
 BLOCK = 1024
@@ -177,8 +177,12 @@
     sent_at = [jnp.where(me + s < n, 0, half) for s in range(n)]
     got_at = [jnp.where(me - s >= 0, 0, half) for s in range(n)]
 
+    source = players
+
     def send(s, start, size):
-        piece = lax.dynamic_slice(players, (0, start), (rows, size))
+        nonlocal source
+        piece = lax.dynamic_slice(source, (0, start), (rows, size))
+        source, piece = lax.optimization_barrier((source, piece))
         return lax.ppermute(piece, "player", ring[s])
 
     early, late, place = [], [], 0
@@ -199,15 +203,18 @@
         place += size
 
     rhs = ((1,), (1,))
-    own_gram = dot(players, players, rhs)
-    own_proj = dot(players, slab, rhs)
+    own_gram = dot(source, source, rhs)
+    own_proj = dot(source, slab, rhs)
     slab_gram = dot(slab, slab, rhs)
     cross = []
     for s in range(1, n):
         total = 0.0
         for place, size, got in early:
             mine = lax.dynamic_slice(players, (0, got_at[s] + place), (rows, size))
-            total = total + dot(mine, got[s - 1], rhs)
+            piece = got[s - 1]
+            if place:
+                total, piece = lax.optimization_barrier((total, piece))
+            total = total + dot(mine, piece, rhs)
         cross.append(total)
 
     if batch >= rows:

time: 438 us -> 425 us (0.970)
  waiting for transfers between devices: 249 us -> 225 us
  local copies, waits for them, and re-layouts: 25.1 us -> 34.1 us
    ppermute x11, waiting for transfers between devices: 221 us -> 197 us  [send(): return lax.ppermute(piece, 'player', ring[s])]
    dynamic_slice x5 -> x11, local copies, waits for them, and re-layouts: 19.4 us -> 28.7 us  [send(): piece = lax.dynamic_slice(source, (0, start), (rows, size))]
  transfers between devices with their start and end apart: 20 -> 20, of which waited for: 14 -> 15; matrix products, arithmetic and copies ran while one was open for 15% -> 18% of each run, Pallas kernels for 18% -> 19%
where the time goes in v2:
time: 425 us; the launch traced here: 423 us
  waiting for transfers between devices  225 us (53%)
  Pallas kernels  82.3 us (19%)
  matrix products  44.3 us (10%)
  local copies, waits for them, and re-layouts  34.1 us (8%)
  starting transfers between devices  27.9 us (7%)
  other arithmetic  9.51 us (2%)
    ppermute x11, waiting for transfers between devices, send(): return lax.ppermute(piece, 'player', ring[s])  197 us
    pallas_call x11, Pallas kernels, update_piece(): pl.pallas_call(functools.partial(update_kernel, count), out_shape=jax.Sha...  70.5 us
    dot_general x7, matrix products, dot(): lax.dot_general(a, b, (contract, ((), ())), precision=precision, preferre...  44.3 us
    dynamic_slice x11, local copies, waits for them, and re-layouts, send(): piece = lax.dynamic_slice(source, (0, start), (rows, size))  28.7 us
    ppermute x4, waiting for transfers between devices, gather_back(): got = lax.ppermute(x, axis, [(i, i ^ step) for i in range(size)])  13 us
    ppermute x11, starting transfers between devices, send(): return lax.ppermute(piece, 'player', ring[s])  12.7 us
    ppermute x4, waiting for transfers between devices, scatter_sum(): got = lax.ppermute(send, axis, [(i, i ^ step) for i in range(size)])  12 us
    pallas_call x1, Pallas kernels, coefficients_of(): pl.pallas_call(functools.partial(coeff_kernel, rows, features), out_shape...  11.8 us
  transfers between devices with their start and end apart: 20, of which 15 were waited for; matrix products, arithmetic and copies ran while one was open for 18% of the time, Pallas kernels for 19%

profile of v2, /device:TPU:0, one launch (start us, length us, event | category | flops | bytes accessed | tf_op | source)
XLA Modules:
  0.0 423.2 jit_solution(5929929658055015985)
XLA Ops:
  6.7 4.6 %constant_dynamic-slice_fusion.8 = bf16[256,8192]{1,0:T(8,128)(2,1)} fusion(bf16[256,32768]{1,0:T(8,128)(2,1)} %w_ref.21, s32[]{:T(128)S(6)} %select_n.197), kind=kLoop, calls=%fused_computation.55 | loop fusion | bytes 8388612 | tf_op jit(solution)/shard_map/dynamic_slice | solution.py:184
  33.8 13.6 %fusion.13 = f32[256,256]{1,0:T(8,128)} fusion(bf16[256,32768]{1,0:T(8,128)(2,1)} %w_ref.21), kind=kOutput, calls=%fused_computation.61 | convolution fusion | flops 4294967296 | bytes 17039360 | tf_op jit(solution)/shard_map/dot_general | solution.py:21
  47.4 10.7 %fusion.14 = f32[256,128]{1,0:T(8,128)S(1)} fusion(bf16[256,32768]{1,0:T(8,128)(2,1)} %w_ref.21, bf16[128,32768]{1,0:T(8,128)(2,1)} %x_ref.21), kind=kOutput, calls=%fused_computation.62 | convolution fusion | flops 2147483648 | bytes 25296896 | tf_op jit(solution)/shard_map/dot_general | solution.py:21
  58.1 8.1 %fusion.15 = f32[128,128]{1,0:T(8,128)S(1)} fusion(bf16[128,32768]{1,0:T(8,128)(2,1)} %x_ref.21), kind=kOutput, calls=%fused_computation.63 | convolution fusion | flops 1073741824 | bytes 8454144 | tf_op jit(solution)/shard_map/dot_general | solution.py:21
  70.3 73.1 %collective-permute-done.3.refs_0_ = bf16[256,8192]{1,0:T(8,128)(2,1)} collective-permute-done((bf16[256,8192]{1,0:T(8,128)(2,1)}, bf16[256,8192]{1,0:T(8,128)(2,1)}, u32[]{:S(2)}, u32[]{:S(2)}) %collective-permute-start.3) | collective-permute-done | bytes 4194336 | tf_op jit(solution)/shard_map/ppermute | solution.py:186
  143.4 4.7 %fusion = f32[256,256]{1,0:T(8,128)S(1)} fusion(bf16[256,8192]{1,0:T(8,128)(2,1)} %collective-permute-done.3.refs_0_, bf16[256,32768]{1,0:T(8,128)(2,1)} %w_ref.21, s32[]{:T(128)S(6)} %select_n.216), kind=kOutput, calls=%fused_computation | convolution fusion | flops 1073741824 | bytes 8650756 | tf_op jit(solution)/shard_map/dot_general | solution.py:21
  148.2 39.2 %collective-permute-done.4.refs_0_ = bf16[256,4096]{1,0:T(8,128)(2,1)S(1)} collective-permute-done((bf16[256,4096]{1,0:T(8,128)(2,1)}, bf16[256,4096]{1,0:T(8,128)(2,1)S(1)}, u32[]{:S(2)}, u32[]{:S(2)}) %collective-permute-start.4) | collective-permute-done | bytes 2097184 | tf_op jit(solution)/shard_map/ppermute | solution.py:186
  195.5 5.2 %collective-permute-done.6 = f32[64,768]{1,0:T(8,128)S(1)} collective-permute-done((f32[64,768]{1,0:T(8,128)S(1)}, f32[64,768]{1,0:T(8,128)S(1)}, u32[]{:S(2)}, u32[]{:S(2)}) %collective-permute-start.6) | collective-permute-done | bytes 196640 | tf_op jit(solution)/shard_map/ppermute | solution.py:40
  228.4 6.3 %collective-permute-done.12 = f32[2,64,768]{2,1,0:T(8,128)S(1)} collective-permute-done((f32[2,64,768]{2,1,0:T(8,128)S(1)}, f32[2,64,768]{2,1,0:T(8,128)S(1)}, u32[]{:S(2)}, u32[]{:S(2)}) %collective-permute-start.12) | collective-permute-done | bytes 393248 | tf_op jit(solution)/shard_map/ppermute | solution.py:51
  252.1 11.8 %coefficients_of.1 = (bf16[512,640]{1,0:T(8,128)(2,1)}, bf16[256,640]{1,0:T(8,128)(2,1)}, f32[512,1]{1,0:T(8,128)}, f32[256,1]{1,0:T(8,128)}) custom-call(f32[640,640]{1,0:T(8,128)} %maximum_maximum_fusion.gram_ref, s32[512,1]{1,0:T(8,128)} %copy.33.down_ref, s32[1,512]{1,0:T(1,128)} %bitcast.55), custom_call_target="tpu_custom_call" | custom-call | flops 5033164800 | bytes 3276800 | tf_op jit(solution)/shard_map/coefficients_of/pallas_call | solution.py:95
  267.6 6.6 %update_piece.12.refs_5_ = bf16[256,32768]{1,0:T(8,128)(2,1)} custom-call(s32[1]{0:T(128)} %bitcast.23.base_ref, bf16[256,32768]{1,0:T(8,128)(2,1)} %w_ref.21, bf16[128,32768]{1,0:T(8,128)(2,1)} %x_ref.21, bf16[256,3072]{1,0:T(8,128)(2,1)} %collective-permute-done.2.refs_0_, ...), custom_call_target="tpu_custom_call", output_to_operand_aliasing={{}: (8, {})} | custom-call | flops 3019898880 | bytes 5505024 | tf_op jit(solution)/shard_map/update_piece/pallas_call | solution.py:144
  274.2 13.5 %update_piece.13.refs_5_ = bf16[256,32768]{1,0:T(8,128)(2,1)} custom-call(s32[1]{0:T(128)} %bitcast.22.base_ref, bf16[256,32768]{1,0:T(8,128)(2,1)} %w_ref.21, bf16[128,32768]{1,0:T(8,128)(2,1)} %x_ref.21, bf16[256,8192]{1,0:T(8,128)(2,1)} %collective-permute-done.3.refs_0_, ...), custom_call_target="tpu_custom_call", output_to_operand_aliasing={{}: (8, {})} | custom-call | flops 8053063680 | bytes 14680064 | tf_op jit(solution)/shard_map/update_piece/pallas_call | solution.py:144
  287.7 8.0 %update_piece.14.refs_5_ = bf16[256,32768]{1,0:T(8,128)(2,1)} custom-call(s32[1]{0:T(128)} %bitcast.21.base_ref, bf16[256,32768]{1,0:T(8,128)(2,1)} %w_ref.21, bf16[128,32768]{1,0:T(8,128)(2,1)} %x_ref.21, bf16[256,4096]{1,0:T(8,128)(2,1)} %copy-done, bf16[512,640]{1,0:T(8,128)(2,1)} %get-tuple-element.59.refs_1_, ...), custom_call_target="tpu_custom_call", output_to_operand_aliasing={{}: (8, {})} | custom-call | flops 4026531840 | bytes 7340032 | tf_op jit(solution)/shard_map/update_piece/pallas_call | solution.py:144
  296.2 5.2 %update_piece.15.refs_5_ = bf16[256,32768]{1,0:T(8,128)(2,1)} custom-call(s32[1]{0:T(128)} %bitcast.20.base_ref, bf16[256,32768]{1,0:T(8,128)(2,1)} %w_ref.21, bf16[128,32768]{1,0:T(8,128)(2,1)} %x_ref.21, bf16[256,2048]{1,0:T(8,128)(2,1)} %collective-permute-done.19.refs_0_, ...), custom_call_target="tpu_custom_call", output_to_operand_aliasing={{}: (8, {})} | custom-call | flops 2013265920 | bytes 3670016 | tf_op jit(solution)/shard_map/update_piece/pallas_call | solution.py:144
  303.0 5.1 %update_piece.16.refs_5_ = bf16[256,32768]{1,0:T(8,128)(2,1)} custom-call(s32[1]{0:T(128)} %bitcast.19.base_ref, bf16[256,32768]{1,0:T(8,128)(2,1)} %w_ref.21, bf16[128,32768]{1,0:T(8,128)(2,1)} %x_ref.21, bf16[256,2048]{1,0:T(8,128)(2,1)} %copy-done.2, bf16[512,640]{1,0:T(8,128)(2,1)} %get-tuple-element.59.refs_1_, ...), custom_call_target="tpu_custom_call", output_to_operand_aliasing={{}: (8, {})} | custom-call | flops 2013265920 | bytes 3670016 | tf_op jit(solution)/shard_map/update_piece/pallas_call | solution.py:144
  308.2 21.2 %collective-permute-done.17.refs_0_ = bf16[256,4096]{1,0:T(8,128)(2,1)} collective-permute-done((bf16[256,4096]{1,0:T(8,128)(2,1)}, bf16[256,4096]{1,0:T(8,128)(2,1)}, u32[]{:S(2)}, u32[]{:S(2)}) %collective-permute-start.17) | collective-permute-done | bytes 2097184 | tf_op jit(solution)/shard_map/ppermute | solution.py:186
  329.4 7.9 %update_piece.17.refs_5_ = bf16[256,32768]{1,0:T(8,128)(2,1)} custom-call(s32[1]{0:T(128)} %bitcast.18.base_ref, bf16[256,32768]{1,0:T(8,128)(2,1)} %w_ref.21, bf16[128,32768]{1,0:T(8,128)(2,1)} %x_ref.21, bf16[256,4096]{1,0:T(8,128)(2,1)} %collective-permute-done.17.refs_0_, ...), custom_call_target="tpu_custom_call", output_to_operand_aliasing={{}: (8, {})} | custom-call | flops 4026531840 | bytes 7340032 | tf_op jit(solution)/shard_map/update_piece/pallas_call | solution.py:144
  337.3 37.0 %collective-permute-done.16.refs_0_ = bf16[256,4096]{1,0:T(8,128)(2,1)} collective-permute-done((bf16[256,4096]{1,0:T(8,128)(2,1)}, bf16[256,4096]{1,0:T(8,128)(2,1)}, u32[]{:S(2)}, u32[]{:S(2)}) %collective-permute-start.16) | collective-permute-done | bytes 2097184 | tf_op jit(solution)/shard_map/ppermute | solution.py:186
  374.3 7.9 %update_piece.18.refs_5_ = bf16[256,32768]{1,0:T(8,128)(2,1)} custom-call(s32[1]{0:T(128)} %bitcast.17.base_ref, bf16[256,32768]{1,0:T(8,128)(2,1)} %w_ref.21, bf16[128,32768]{1,0:T(8,128)(2,1)} %x_ref.21, bf16[256,4096]{1,0:T(8,128)(2,1)} %collective-permute-done.16.refs_0_, ...), custom_call_target="tpu_custom_call", output_to_operand_aliasing={{}: (8, {})} | custom-call | flops 4026531840 | bytes 7340032 | tf_op jit(solution)/shard_map/update_piece/pallas_call | solution.py:144
  382.3 14.6 %collective-permute-done.15.refs_0_ = bf16[256,2048]{1,0:T(8,128)(2,1)} collective-permute-done((bf16[256,2048]{1,0:T(8,128)(2,1)}, bf16[256,2048]{1,0:T(8,128)(2,1)}, u32[]{:S(2)}, u32[]{:S(2)}) %collective-permute-start.15) | collective-permute-done | bytes 1048608 | tf_op jit(solution)/shard_map/ppermute | solution.py:186
  396.8 5.1 %update_piece.19.refs_5_ = bf16[256,32768]{1,0:T(8,128)(2,1)} custom-call(s32[1]{0:T(128)} %bitcast.16.base_ref, bf16[256,32768]{1,0:T(8,128)(2,1)} %w_ref.21, bf16[128,32768]{1,0:T(8,128)(2,1)} %x_ref.21, bf16[256,2048]{1,0:T(8,128)(2,1)} %collective-permute-done.15.refs_0_, ...), custom_call_target="tpu_custom_call", output_to_operand_aliasing={{}: (8, {})} | custom-call | flops 2013265920 | bytes 3670016 | tf_op jit(solution)/shard_map/update_piece/pallas_call | solution.py:144
  401.9 6.0 %collective-permute-done.14.refs_0_ = bf16[256,1024]{1,0:T(8,128)(2,1)S(1)} collective-permute-done((bf16[256,1024]{1,0:T(8,128)(2,1)S(1)}, bf16[256,1024]{1,0:T(8,128)(2,1)S(1)}, u32[]{:S(2)}, u32[]{:S(2)}) %collective-permute-start.14) | collective-permute-done | bytes 524320 | tf_op jit(solution)/shard_map/ppermute | solution.py:186
  412.5 6.3 %collective-permute-done.refs_0_ = bf16[256,1024]{1,0:T(8,128)(2,1)S(1)} collective-permute-done((bf16[256,1024]{1,0:T(8,128)(2,1)S(1)}, bf16[256,1024]{1,0:T(8,128)(2,1)S(1)}, u32[]{:S(2)}, u32[]{:S(2)}) %collective-permute-start) | collective-permute-done | bytes 524320 | tf_op jit(solution)/shard_map/ppermute | solution.py:186
  419.5 3.7 update_piece.21
  (100 shorter events, 97.5 us)
Async XLA Ops:
  3.8 64.0 %collective-permute-start.2 = (bf16[256,3072]{1,0:T(8,128)(2,1)}, bf16[256,3072]{1,0:T(8,128)(2,1)}, u32[]{:S(2)}, u32[]{:S(2)}) collective-permute-start(bf16[256,3072]{1,0:T(8,128)(2,1)} %constant_dynamic-slice_fusion.9), channel_id=1, source_target_pairs={{0,16},{16,0},{1,17},{17,1},{2,18},{18,2},{3,19},{19,3},{4,20},{20... | collective-permute-start | bytes 4718600 | tf_op jit(solution)/shard_map/ppermute | solution.py:186
  6.7 59.4 %collective-permute-start.1 = (bf16[256,1024]{1,0:T(8,128)(2,1)S(1)}, bf16[256,1024]{1,0:T(8,128)(2,1)S(1)}, u32[]{:S(2)}, u32[]{:S(2)}) collective-permute-start(bf16[256,1024]{1,0:T(8,128)(2,1)S(1)} %constant_dynamic-slice_fusion.10), channel_id=1, source_target_pairs={{0,16},{16,0},{1,17},{17,1},{2,18},{18,2},{3,19},{19,3},{4,20},{20... | collective-permute-start | bytes 1572872 | tf_op jit(solution)/shard_map/ppermute | solution.py:186
  11.4 132.0 %collective-permute-start.3 = (bf16[256,8192]{1,0:T(8,128)(2,1)}, bf16[256,8192]{1,0:T(8,128)(2,1)}, u32[]{:S(2)}, u32[]{:S(2)}) collective-permute-start(bf16[256,8192]{1,0:T(8,128)(2,1)} %constant_dynamic-slice_fusion.8), channel_id=1, source_target_pairs={{0,16},{16,0},{1,17},{17,1},{2,18},{18,2},{3,19},{19,3},{4,20},{20... | collective-permute-start | bytes 12582920 | tf_op jit(solution)/shard_map/ppermute | solution.py:186
  16.6 170.8 %collective-permute-start.4 = (bf16[256,4096]{1,0:T(8,128)(2,1)}, bf16[256,4096]{1,0:T(8,128)(2,1)S(1)}, u32[]{:S(2)}, u32[]{:S(2)}) collective-permute-start(bf16[256,4096]{1,0:T(8,128)(2,1)} %constant_dynamic-slice_fusion.7), channel_id=1, source_target_pairs={{0,16},{16,0},{1,17},{17,1},{2,18},{18,2},{3,19},{19,3},{4,20},{20... | collective-permute-start | bytes 6291464 | tf_op jit(solution)/shard_map/ppermute | solution.py:186
  66.2 124.3 %copy-start.1 = (bf16[256,1024]{1,0:T(8,128)(2,1)}, bf16[256,1024]{1,0:T(8,128)(2,1)S(1)}, u32[]{:S(2)}) copy-start(bf16[256,1024]{1,0:T(8,128)(2,1)S(1)} %collective-permute-done.1.refs_0_) | copy-start | bytes 1572868
  70.3 120.3 %copy-start.7 = (f32[256,256]{1,0:T(8,128)S(1)}, f32[256,256]{1,0:T(8,128)}, u32[]{:S(2)}) copy-start(f32[256,256]{1,0:T(8,128)} %fusion.13) | copy-start | bytes 786436
  187.4 48.3 %copy-start = (bf16[256,4096]{1,0:T(8,128)(2,1)}, bf16[256,4096]{1,0:T(8,128)(2,1)S(1)}, u32[]{:S(2)}) copy-start(bf16[256,4096]{1,0:T(8,128)(2,1)S(1)} %collective-permute-done.4.refs_0_) | copy-start | bytes 6291460
  190.7 1.9 collective-permute-start.5
  193.7 7.0 %collective-permute-start.6 = (f32[64,768]{1,0:T(8,128)S(1)}, f32[64,768]{1,0:T(8,128)S(1)}, u32[]{:S(2)}, u32[]{:S(2)}) collective-permute-start(f32[64,768]{1,0:T(8,128)S(1)} %slice_select_fusion.1), channel_id=1, source_target_pairs={{0,2},{1,3},{2,0},{3,1},{4,6},{5,7},{6,4},{7,5},{8,10},{9,11},{10,... | collective-permute-start | bytes 589832 | tf_op jit(solution)/shard_map/ppermute | solution.py:40
  200.8 4.7 %collective-permute-start.7 = (f32[32,768]{1,0:T(8,128)S(1)}, f32[32,768]{1,0:T(8,128)S(1)}, u32[]{:S(2)}, u32[]{:S(2)}) collective-permute-start(f32[32,768]{1,0:T(8,128)S(1)} %slice_select_fusion.2), channel_id=1, source_target_pairs={{0,4},{1,5},{2,6},{3,7},{4,0},{5,1},{6,2},{7,3},{8,12},{9,13},{10,... | collective-permute-start | bytes 294920 | tf_op jit(solution)/shard_map/ppermute | solution.py:40
  205.5 5.1 %collective-permute-start.8 = (f32[16,768]{1,0:T(8,128)S(1)}, f32[16,768]{1,0:T(8,128)S(1)}, u32[]{:S(2)}, u32[]{:S(2)}) collective-permute-start(f32[16,768]{1,0:T(8,128)S(1)} %slice_select_fusion.3), channel_id=1, source_target_pairs={{0,8},{1,9},{2,10},{3,11},{4,12},{5,13},{6,14},{7,15},{8,0},{9,1},... | collective-permute-start | bytes 147464 | tf_op jit(solution)/shard_map/ppermute | solution.py:40
  210.6 4.2 collective-permute-start.9
  214.7 6.0 %collective-permute-start.10 = (f32[2,16,768]{2,1,0:T(8,128)S(1)}, f32[2,16,768]{2,1,0:T(8,128)S(1)}, u32[]{:S(2)}, u32[]{:S(2)}) collective-permute-start(f32[2,16,768]{2,1,0:T(8,128)S(1)} %pad_maximum_fusion.10), channel_id=1, source_target_pairs={{0,8},{1,9},{2,10},{3,11},{4,12},{5,13},{6,14},{7,15},{8,0},{9,1},... | collective-permute-start | bytes 294920 | tf_op jit(solution)/shard_map/ppermute | solution.py:51
  220.8 6.0 %collective-permute-start.11 = (f32[2,32,768]{2,1,0:T(8,128)S(1)}, f32[2,32,768]{2,1,0:T(8,128)S(1)}, u32[]{:S(2)}, u32[]{:S(2)}) collective-permute-start(f32[2,32,768]{2,1,0:T(8,128)S(1)} %pad_maximum_fusion.7), channel_id=1, source_target_pairs={{0,4},{1,5},{2,6},{3,7},{4,0},{5,1},{6,2},{7,3},{8,12},{9,13},{10,... | collective-permute-start | bytes 589832 | tf_op jit(solution)/shard_map/ppermute | solution.py:51
  226.8 7.8 %collective-permute-start.12 = (f32[2,64,768]{2,1,0:T(8,128)S(1)}, f32[2,64,768]{2,1,0:T(8,128)S(1)}, u32[]{:S(2)}, u32[]{:S(2)}) collective-permute-start(f32[2,64,768]{2,1,0:T(8,128)S(1)} %pad_maximum_fusion.2), channel_id=1, source_target_pairs={{0,2},{1,3},{2,0},{3,1},{4,6},{5,7},{6,4},{7,5},{8,10},{9,11},{10,... | collective-permute-start | bytes 1179656 | tf_op jit(solution)/shard_map/ppermute | solution.py:51
  235.6 5.0 %collective-permute-start.13 = (f32[2,128,768]{2,1,0:T(8,128)}, f32[2,128,768]{2,1,0:T(8,128)}, u32[]{:S(2)}, u32[]{:S(2)}) collective-permute-start(f32[2,128,768]{2,1,0:T(8,128)} %pad_maximum_fusion), channel_id=1, source_target_pairs={{0,1},{1,0},{2,3},{3,2},{4,5},{5,4},{6,7},{7,6},{8,9},{9,8},{10,11... | collective-permute-start | bytes 2359304 | tf_op jit(solution)/shard_map/ppermute | solution.py:51
  235.6 60.0 %collective-permute-start.19 = (bf16[256,2048]{1,0:T(8,128)(2,1)}, bf16[256,2048]{1,0:T(8,128)(2,1)}, u32[]{:S(2)}, u32[]{:S(2)}) collective-permute-start(bf16[256,2048]{1,0:T(8,128)(2,1)} %constant_dynamic-slice_fusion.6), channel_id=1, source_target_pairs={{0,16},{16,0},{1,17},{17,1},{2,18},{18,2},{3,19},{19,3},{4,20},{20... | collective-permute-start | bytes 3145736 | tf_op jit(solution)/shard_map/ppermute | solution.py:186
  237.1 64.3 %collective-permute-start.18 = (bf16[256,2048]{1,0:T(8,128)(2,1)}, bf16[256,2048]{1,0:T(8,128)(2,1)S(1)}, u32[]{:S(2)}, u32[]{:S(2)}) collective-permute-start(bf16[256,2048]{1,0:T(8,128)(2,1)} %constant_dynamic-slice_fusion.5), channel_id=1, source_target_pairs={{0,16},{16,0},{1,17},{17,1},{2,18},{18,2},{3,19},{19,3},{4,20},{20... | collective-permute-start | bytes 3145736 | tf_op jit(solution)/shard_map/ppermute | solution.py:186
  237.7 91.7 %collective-permute-start.17 = (bf16[256,4096]{1,0:T(8,128)(2,1)}, bf16[256,4096]{1,0:T(8,128)(2,1)}, u32[]{:S(2)}, u32[]{:S(2)}) collective-permute-start(bf16[256,4096]{1,0:T(8,128)(2,1)} %constant_dynamic-slice_fusion.4), channel_id=1, source_target_pairs={{0,16},{16,0},{1,17},{17,1},{2,18},{18,2},{3,19},{19,3},{4,20},{20... | collective-permute-start | bytes 6291464 | tf_op jit(solution)/shard_map/ppermute | solution.py:186
  239.2 135.2 %collective-permute-start.16 = (bf16[256,4096]{1,0:T(8,128)(2,1)}, bf16[256,4096]{1,0:T(8,128)(2,1)}, u32[]{:S(2)}, u32[]{:S(2)}) collective-permute-start(bf16[256,4096]{1,0:T(8,128)(2,1)} %constant_dynamic-slice_fusion.3), channel_id=1, source_target_pairs={{0,16},{16,0},{1,17},{17,1},{2,18},{18,2},{3,19},{19,3},{4,20},{20... | collective-permute-start | bytes 6291464 | tf_op jit(solution)/shard_map/ppermute | solution.py:186
  239.7 12.4 %copy-start.8 = (s32[512]{0:T(512)}, s32[512]{0:T(512)S(1)}, u32[]{:S(2)}) copy-start(s32[512]{0:T(512)S(1)} %pad_add_fusion) | copy-start | bytes 6148
  240.6 156.2 %collective-permute-start.15 = (bf16[256,2048]{1,0:T(8,128)(2,1)}, bf16[256,2048]{1,0:T(8,128)(2,1)}, u32[]{:S(2)}, u32[]{:S(2)}) collective-permute-start(bf16[256,2048]{1,0:T(8,128)(2,1)} %constant_dynamic-slice_fusion.2), channel_id=1, source_target_pairs={{0,16},{16,0},{1,17},{17,1},{2,18},{18,2},{3,19},{19,3},{4,20},{20... | collective-permute-start | bytes 3145736 | tf_op jit(solution)/shard_map/ppermute | solution.py:186
  295.6 112.3 %collective-permute-start.14 = (bf16[256,1024]{1,0:T(8,128)(2,1)S(1)}, bf16[256,1024]{1,0:T(8,128)(2,1)S(1)}, u32[]{:S(2)}, u32[]{:S(2)}) collective-permute-start(bf16[256,1024]{1,0:T(8,128)(2,1)S(1)} %copy-done.5), channel_id=1, source_target_pairs={{0,16},{16,0},{1,17},{17,1},{2,18},{18,2},{3,19},{19,3},{4,20},{20... | collective-permute-start | bytes 1572872 | tf_op jit(solution)/shard_map/ppermute | solution.py:186
  301.5 117.3 %collective-permute-start = (bf16[256,1024]{1,0:T(8,128)(2,1)S(1)}, bf16[256,1024]{1,0:T(8,128)(2,1)S(1)}, u32[]{:S(2)}, u32[]{:S(2)}) collective-permute-start(bf16[256,1024]{1,0:T(8,128)(2,1)S(1)} %copy-done.6), channel_id=1, source_target_pairs={{0,16},{16,0},{1,17},{17,1},{2,18},{18,2},{3,19},{19,3},{4,20},{20... | collective-permute-start | bytes 1572872 | tf_op jit(solution)/shard_map/ppermute | solution.py:186
  (5 other events, 16.3 us)

commit v3 on v2

--- a/solution.py
+++ b/solution.py
@@ -8,9 +8,9 @@
 from jax.sharding import PartitionSpec as P
 
 
-EARLY = (1, 3, 8, 4)
-LATE = (2, 2, 4, 4, 2, 1, 1)
-UNIT = 32
+EARLY = (1, 7, 16, 8)
+LATE = (4, 4, 8, 8, 4, 2, 1, 1)
+UNIT = 64
 BLOCK = 1024
 
 

time: 425 us -> 425 us (level)
  waiting for transfers between devices: 225 us -> 206 us
  Pallas kernels: 82.3 us -> 97.3 us
    ppermute x11 -> x12, waiting for transfers between devices: 197 us -> 179 us  [send(): return lax.ppermute(piece, 'player', ring[s])]
    pallas_call x11 -> x12, Pallas kernels: 70.5 us -> 85.5 us  [update_piece(): pl.pallas_call(functools.partial(update_kernel, count), out_shape=jax.Sha...]
    dynamic_slice x11 -> x12, local copies, waits for them, and re-layouts: 28.7 us -> 30.3 us  [send(): piece = lax.dynamic_slice(source, (0, start), (rows, size))]
    ppermute x11 -> x12, starting transfers between devices: 12.7 us -> 14.2 us  [send(): return lax.ppermute(piece, 'player', ring[s])]
  transfers between devices with their start and end apart: 20 -> 21, of which waited for: 15 -> 16; matrix products, arithmetic and copies ran while one was open for 18% -> 18% of each run, Pallas kernels for 19% -> 22%
where the time goes in v3:
time: 425 us; the launch traced here: 422 us
  waiting for transfers between devices  206 us (48%)
  Pallas kernels  97.3 us (23%)
  matrix products  43.6 us (10%)
  local copies, waits for them, and re-layouts  36.3 us (9%)
  starting transfers between devices  29.5 us (7%)
  other arithmetic  9.52 us (2%)
    ppermute x12, waiting for transfers between devices, send(): return lax.ppermute(piece, 'player', ring[s])  179 us
    pallas_call x12, Pallas kernels, update_piece(): pl.pallas_call(functools.partial(update_kernel, count), out_shape=jax.Sha...  85.5 us
    dot_general x7, matrix products, dot(): lax.dot_general(a, b, (contract, ((), ())), precision=precision, preferre...  43.6 us
    dynamic_slice x12, local copies, waits for them, and re-layouts, send(): piece = lax.dynamic_slice(source, (0, start), (rows, size))  30.3 us
    ppermute x12, starting transfers between devices, send(): return lax.ppermute(piece, 'player', ring[s])  14.2 us
    ppermute x4, waiting for transfers between devices, gather_back(): got = lax.ppermute(x, axis, [(i, i ^ step) for i in range(size)])  13 us
    ppermute x4, waiting for transfers between devices, scatter_sum(): got = lax.ppermute(send, axis, [(i, i ^ step) for i in range(size)])  12 us
    pallas_call x1, Pallas kernels, coefficients_of(): pl.pallas_call(functools.partial(coeff_kernel, rows, features), out_shape...  11.8 us
  transfers between devices with their start and end apart: 21, of which 16 were waited for; matrix products, arithmetic and copies ran while one was open for 18% of the time, Pallas kernels for 22%

profile of v3, /device:TPU:0, one launch (start us, length us, event | category | flops | bytes accessed | tf_op | source)
XLA Modules:
  0.0 422.5 jit_solution(5002785304873464127)
XLA Ops:
  6.8 4.6 %constant_dynamic-slice_fusion.9 = bf16[256,8192]{1,0:T(8,128)(2,1)} fusion(bf16[256,32768]{1,0:T(8,128)(2,1)} %w_ref.23, s32[]{:T(128)S(6)} %select_n.203), kind=kLoop, calls=%fused_computation.56 | loop fusion | bytes 8388612 | tf_op jit(solution)/shard_map/dynamic_slice | solution.py:184
  35.3 12.9 %fusion.13 = f32[256,256]{1,0:T(8,128)S(1)} fusion(bf16[256,32768]{1,0:T(8,128)(2,1)} %w_ref.23), kind=kOutput, calls=%fused_computation.62 | convolution fusion | flops 4294967296 | bytes 17039360 | tf_op jit(solution)/shard_map/dot_general | solution.py:21
  48.2 10.7 %fusion.14 = f32[256,128]{1,0:T(8,128)S(1)} fusion(bf16[256,32768]{1,0:T(8,128)(2,1)} %w_ref.23, bf16[128,32768]{1,0:T(8,128)(2,1)} %x_ref.23), kind=kOutput, calls=%fused_computation.63 | convolution fusion | flops 2147483648 | bytes 25296896 | tf_op jit(solution)/shard_map/dot_general | solution.py:21
  58.9 8.1 %fusion.15 = f32[128,128]{1,0:T(8,128)S(1)} fusion(bf16[128,32768]{1,0:T(8,128)(2,1)} %x_ref.23), kind=kOutput, calls=%fused_computation.64 | convolution fusion | flops 1073741824 | bytes 8454144 | tf_op jit(solution)/shard_map/dot_general | solution.py:21
  71.1 72.4 %collective-permute-done.3.refs_0_ = bf16[256,8192]{1,0:T(8,128)(2,1)} collective-permute-done((bf16[256,8192]{1,0:T(8,128)(2,1)}, bf16[256,8192]{1,0:T(8,128)(2,1)}, u32[]{:S(2)}, u32[]{:S(2)}) %collective-permute-start.3) | collective-permute-done | bytes 4194336 | tf_op jit(solution)/shard_map/ppermute | solution.py:186
  143.5 4.7 %fusion = f32[256,256]{1,0:T(8,128)S(1)} fusion(bf16[256,8192]{1,0:T(8,128)(2,1)} %collective-permute-done.3.refs_0_, bf16[256,32768]{1,0:T(8,128)(2,1)} %w_ref.23, s32[]{:T(128)S(6)} %select_n.223), kind=kOutput, calls=%fused_computation | convolution fusion | flops 1073741824 | bytes 8650756 | tf_op jit(solution)/shard_map/dot_general | solution.py:21
  148.3 39.2 %collective-permute-done.4.refs_0_ = bf16[256,4096]{1,0:T(8,128)(2,1)S(1)} collective-permute-done((bf16[256,4096]{1,0:T(8,128)(2,1)}, bf16[256,4096]{1,0:T(8,128)(2,1)S(1)}, u32[]{:S(2)}, u32[]{:S(2)}) %collective-permute-start.4) | collective-permute-done | bytes 2097184 | tf_op jit(solution)/shard_map/ppermute | solution.py:186
  195.6 5.2 %collective-permute-done.6 = f32[64,768]{1,0:T(8,128)S(1)} collective-permute-done((f32[64,768]{1,0:T(8,128)S(1)}, f32[64,768]{1,0:T(8,128)S(1)}, u32[]{:S(2)}, u32[]{:S(2)}) %collective-permute-start.6) | collective-permute-done | bytes 196640 | tf_op jit(solution)/shard_map/ppermute | solution.py:40
  223.2 3.6 collective-permute-done.11
  228.5 6.3 %collective-permute-done.12 = f32[2,64,768]{2,1,0:T(8,128)S(1)} collective-permute-done((f32[2,64,768]{2,1,0:T(8,128)S(1)}, f32[2,64,768]{2,1,0:T(8,128)S(1)}, u32[]{:S(2)}, u32[]{:S(2)}) %collective-permute-start.12) | collective-permute-done | bytes 393248 | tf_op jit(solution)/shard_map/ppermute | solution.py:51
  252.2 11.8 %coefficients_of.1 = (bf16[512,640]{1,0:T(8,128)(2,1)}, bf16[256,640]{1,0:T(8,128)(2,1)}, f32[512,1]{1,0:T(8,128)}, f32[256,1]{1,0:T(8,128)}) custom-call(f32[640,640]{1,0:T(8,128)} %maximum_maximum_fusion.gram_ref, s32[512,1]{1,0:T(8,128)} %copy.34.down_ref, s32[1,512]{1,0:T(1,128)} %bitcast.56), custom_call_target="tpu_custom_call" | custom-call | flops 5033164800 | bytes 3276800 | tf_op jit(solution)/shard_map/coefficients_of/pallas_call | solution.py:95
  266.9 8.8 %update_piece.13.refs_5_ = bf16[256,32768]{1,0:T(8,128)(2,1)} custom-call(s32[1]{0:T(128)} %bitcast.24.base_ref, bf16[256,32768]{1,0:T(8,128)(2,1)} %w_ref.23, bf16[128,32768]{1,0:T(8,128)(2,1)} %x_ref.23, bf16[256,3584]{1,0:T(8,128)(2,1)} %collective-permute-done.2.refs_0_, ...), custom_call_target="tpu_custom_call", output_to_operand_aliasing={{}: (8, {})} | custom-call | flops 3523215360 | bytes 6422528 | tf_op jit(solution)/shard_map/update_piece/pallas_call | solution.py:144
  275.8 17.6 %update_piece.14.refs_5_ = bf16[256,32768]{1,0:T(8,128)(2,1)} custom-call(s32[1]{0:T(128)} %bitcast.23.base_ref, bf16[256,32768]{1,0:T(8,128)(2,1)} %w_ref.23, bf16[128,32768]{1,0:T(8,128)(2,1)} %x_ref.23, bf16[256,8192]{1,0:T(8,128)(2,1)} %collective-permute-done.3.refs_0_, ...), custom_call_target="tpu_custom_call", output_to_operand_aliasing={{}: (8, {})} | custom-call | flops 8053063680 | bytes 14680064 | tf_op jit(solution)/shard_map/update_piece/pallas_call | solution.py:144
  293.4 9.8 %update_piece.15.refs_5_ = bf16[256,32768]{1,0:T(8,128)(2,1)} custom-call(s32[1]{0:T(128)} %bitcast.22.base_ref, bf16[256,32768]{1,0:T(8,128)(2,1)} %w_ref.23, bf16[128,32768]{1,0:T(8,128)(2,1)} %x_ref.23, bf16[256,4096]{1,0:T(8,128)(2,1)} %copy-done, bf16[512,640]{1,0:T(8,128)(2,1)} %get-tuple-element.62.refs_1_, ...), custom_call_target="tpu_custom_call", output_to_operand_aliasing={{}: (8, {})} | custom-call | flops 4026531840 | bytes 7340032 | tf_op jit(solution)/shard_map/update_piece/pallas_call | solution.py:144
  303.7 5.8 %update_piece.16.refs_5_ = bf16[256,32768]{1,0:T(8,128)(2,1)} custom-call(s32[1]{0:T(128)} %bitcast.21.base_ref, bf16[256,32768]{1,0:T(8,128)(2,1)} %w_ref.23, bf16[128,32768]{1,0:T(8,128)(2,1)} %x_ref.23, bf16[256,2048]{1,0:T(8,128)(2,1)} %collective-permute-done.20.refs_0_, ...), custom_call_target="tpu_custom_call", output_to_operand_aliasing={{}: (8, {})} | custom-call | flops 2013265920 | bytes 3670016 | tf_op jit(solution)/shard_map/update_piece/pallas_call | solution.py:144
  311.1 5.8 %update_piece.17.refs_5_ = bf16[256,32768]{1,0:T(8,128)(2,1)} custom-call(s32[1]{0:T(128)} %bitcast.20.base_ref, bf16[256,32768]{1,0:T(8,128)(2,1)} %w_ref.23, bf16[128,32768]{1,0:T(8,128)(2,1)} %x_ref.23, bf16[256,2048]{1,0:T(8,128)(2,1)} %copy-done.1, bf16[512,640]{1,0:T(8,128)(2,1)} %get-tuple-element.62.refs_1_, ...), custom_call_target="tpu_custom_call", output_to_operand_aliasing={{}: (8, {})} | custom-call | flops 2013265920 | bytes 3670016 | tf_op jit(solution)/shard_map/update_piece/pallas_call | solution.py:144
  316.9 12.6 %collective-permute-done.18.refs_0_ = bf16[256,4096]{1,0:T(8,128)(2,1)} collective-permute-done((bf16[256,4096]{1,0:T(8,128)(2,1)}, bf16[256,4096]{1,0:T(8,128)(2,1)}, u32[]{:S(2)}, u32[]{:S(2)}) %collective-permute-start.18) | collective-permute-done | bytes 2097184 | tf_op jit(solution)/shard_map/ppermute | solution.py:186
  331.0 9.7 %update_piece.18.refs_5_ = bf16[256,32768]{1,0:T(8,128)(2,1)} custom-call(s32[1]{0:T(128)} %bitcast.19.base_ref, bf16[256,32768]{1,0:T(8,128)(2,1)} %w_ref.23, bf16[128,32768]{1,0:T(8,128)(2,1)} %x_ref.23, bf16[256,4096]{1,0:T(8,128)(2,1)} %collective-permute-done.18.refs_0_, ...), custom_call_target="tpu_custom_call", output_to_operand_aliasing={{}: (8, {})} | custom-call | flops 4026531840 | bytes 7340032 | tf_op jit(solution)/shard_map/update_piece/pallas_call | solution.py:144
  340.7 33.8 %collective-permute-done.17.refs_0_ = bf16[256,4096]{1,0:T(8,128)(2,1)} collective-permute-done((bf16[256,4096]{1,0:T(8,128)(2,1)}, bf16[256,4096]{1,0:T(8,128)(2,1)}, u32[]{:S(2)}, u32[]{:S(2)}) %collective-permute-start.17) | collective-permute-done | bytes 2097184 | tf_op jit(solution)/shard_map/ppermute | solution.py:186
  374.4 9.7 %update_piece.19.refs_5_ = bf16[256,32768]{1,0:T(8,128)(2,1)} custom-call(s32[1]{0:T(128)} %bitcast.18.base_ref, bf16[256,32768]{1,0:T(8,128)(2,1)} %w_ref.23, bf16[128,32768]{1,0:T(8,128)(2,1)} %x_ref.23, bf16[256,4096]{1,0:T(8,128)(2,1)} %collective-permute-done.17.refs_0_, ...), custom_call_target="tpu_custom_call", output_to_operand_aliasing={{}: (8, {})} | custom-call | flops 4026531840 | bytes 7340032 | tf_op jit(solution)/shard_map/update_piece/pallas_call | solution.py:144
  384.1 12.8 %collective-permute-done.16.refs_0_ = bf16[256,2048]{1,0:T(8,128)(2,1)} collective-permute-done((bf16[256,2048]{1,0:T(8,128)(2,1)}, bf16[256,2048]{1,0:T(8,128)(2,1)}, u32[]{:S(2)}, u32[]{:S(2)}) %collective-permute-start.16) | collective-permute-done | bytes 1048608 | tf_op jit(solution)/shard_map/ppermute | solution.py:186
  396.9 5.7 %update_piece.20.refs_5_ = bf16[256,32768]{1,0:T(8,128)(2,1)} custom-call(s32[1]{0:T(128)} %bitcast.17.base_ref, bf16[256,32768]{1,0:T(8,128)(2,1)} %w_ref.23, bf16[128,32768]{1,0:T(8,128)(2,1)} %x_ref.23, bf16[256,2048]{1,0:T(8,128)(2,1)} %collective-permute-done.16.refs_0_, ...), custom_call_target="tpu_custom_call", output_to_operand_aliasing={{}: (8, {})} | custom-call | flops 2013265920 | bytes 3670016 | tf_op jit(solution)/shard_map/update_piece/pallas_call | solution.py:144
  402.7 5.4 %collective-permute-done.15.refs_0_ = bf16[256,1024]{1,0:T(8,128)(2,1)S(1)} collective-permute-done((bf16[256,1024]{1,0:T(8,128)(2,1)S(1)}, bf16[256,1024]{1,0:T(8,128)(2,1)S(1)}, u32[]{:S(2)}, u32[]{:S(2)}) %collective-permute-start.15) | collective-permute-done | bytes 524320 | tf_op jit(solution)/shard_map/ppermute | solution.py:186
  408.8 3.8 update_piece.21.refs_5_
  (106 shorter events, 101.4 us)
Async XLA Ops:
  3.9 64.5 %collective-permute-start.2 = (bf16[256,3584]{1,0:T(8,128)(2,1)}, bf16[256,3584]{1,0:T(8,128)(2,1)}, u32[]{:S(2)}, u32[]{:S(2)}) collective-permute-start(bf16[256,3584]{1,0:T(8,128)(2,1)} %constant_dynamic-slice_fusion.10), channel_id=1, source_target_pairs={{0,16},{16,0},{1,17},{17,1},{2,18},{18,2},{3,19},{19,3},{4,20},{20... | collective-permute-start | bytes 5505032 | tf_op jit(solution)/shard_map/ppermute | solution.py:186
  6.8 60.2 %collective-permute-start.1 = (bf16[256,512]{1,0:T(8,128)(2,1)S(1)}, bf16[256,512]{1,0:T(8,128)(2,1)S(1)}, u32[]{:S(2)}, u32[]{:S(2)}) collective-permute-start(bf16[256,512]{1,0:T(8,128)(2,1)S(1)} %constant_dynamic-slice_fusion.11), channel_id=1, source_target_pairs={{0,16},{16,0},{1,17},{17,1},{2,18},{18,2},{3,19},{19,3},{4,20},{20... | collective-permute-start | bytes 786440 | tf_op jit(solution)/shard_map/ppermute | solution.py:186
  11.5 132.0 %collective-permute-start.3 = (bf16[256,8192]{1,0:T(8,128)(2,1)}, bf16[256,8192]{1,0:T(8,128)(2,1)}, u32[]{:S(2)}, u32[]{:S(2)}) collective-permute-start(bf16[256,8192]{1,0:T(8,128)(2,1)} %constant_dynamic-slice_fusion.9), channel_id=1, source_target_pairs={{0,16},{16,0},{1,17},{17,1},{2,18},{18,2},{3,19},{19,3},{4,20},{20... | collective-permute-start | bytes 12582920 | tf_op jit(solution)/shard_map/ppermute | solution.py:186
  16.7 170.8 %collective-permute-start.4 = (bf16[256,4096]{1,0:T(8,128)(2,1)}, bf16[256,4096]{1,0:T(8,128)(2,1)S(1)}, u32[]{:S(2)}, u32[]{:S(2)}) collective-permute-start(bf16[256,4096]{1,0:T(8,128)(2,1)} %constant_dynamic-slice_fusion.8), channel_id=1, source_target_pairs={{0,16},{16,0},{1,17},{17,1},{2,18},{18,2},{3,19},{19,3},{4,20},{20... | collective-permute-start | bytes 6291464 | tf_op jit(solution)/shard_map/ppermute | solution.py:186
  67.0 123.6 %copy-start.2 = (bf16[256,512]{1,0:T(8,128)(2,1)}, bf16[256,512]{1,0:T(8,128)(2,1)S(1)}, u32[]{:S(2)}) copy-start(bf16[256,512]{1,0:T(8,128)(2,1)S(1)} %collective-permute-done.1.refs_0_) | copy-start | bytes 786436
  187.5 48.2 %copy-start = (bf16[256,4096]{1,0:T(8,128)(2,1)}, bf16[256,4096]{1,0:T(8,128)(2,1)S(1)}, u32[]{:S(2)}) copy-start(bf16[256,4096]{1,0:T(8,128)(2,1)S(1)} %collective-permute-done.4.refs_0_) | copy-start | bytes 6291460
  190.7 1.9 collective-permute-start.5
  193.8 7.0 %collective-permute-start.6 = (f32[64,768]{1,0:T(8,128)S(1)}, f32[64,768]{1,0:T(8,128)S(1)}, u32[]{:S(2)}, u32[]{:S(2)}) collective-permute-start(f32[64,768]{1,0:T(8,128)S(1)} %slice_select_fusion.1), channel_id=1, source_target_pairs={{0,2},{1,3},{2,0},{3,1},{4,6},{5,7},{6,4},{7,5},{8,10},{9,11},{10,... | collective-permute-start | bytes 589832 | tf_op jit(solution)/shard_map/ppermute | solution.py:40
  200.9 4.7 %collective-permute-start.7 = (f32[32,768]{1,0:T(8,128)S(1)}, f32[32,768]{1,0:T(8,128)S(1)}, u32[]{:S(2)}, u32[]{:S(2)}) collective-permute-start(f32[32,768]{1,0:T(8,128)S(1)} %slice_select_fusion.2), channel_id=1, source_target_pairs={{0,4},{1,5},{2,6},{3,7},{4,0},{5,1},{6,2},{7,3},{8,12},{9,13},{10,... | collective-permute-start | bytes 294920 | tf_op jit(solution)/shard_map/ppermute | solution.py:40
  205.6 5.1 %collective-permute-start.8 = (f32[16,768]{1,0:T(8,128)S(1)}, f32[16,768]{1,0:T(8,128)S(1)}, u32[]{:S(2)}, u32[]{:S(2)}) collective-permute-start(f32[16,768]{1,0:T(8,128)S(1)} %slice_select_fusion.3), channel_id=1, source_target_pairs={{0,8},{1,9},{2,10},{3,11},{4,12},{5,13},{6,14},{7,15},{8,0},{9,1},... | collective-permute-start | bytes 147464 | tf_op jit(solution)/shard_map/ppermute | solution.py:40
  210.6 4.2 collective-permute-start.9
  214.8 6.0 %collective-permute-start.10 = (f32[2,16,768]{2,1,0:T(8,128)S(1)}, f32[2,16,768]{2,1,0:T(8,128)S(1)}, u32[]{:S(2)}, u32[]{:S(2)}) collective-permute-start(f32[2,16,768]{2,1,0:T(8,128)S(1)} %pad_maximum_fusion.10), channel_id=1, source_target_pairs={{0,8},{1,9},{2,10},{3,11},{4,12},{5,13},{6,14},{7,15},{8,0},{9,1},... | collective-permute-start | bytes 294920 | tf_op jit(solution)/shard_map/ppermute | solution.py:51
  220.8 6.0 %collective-permute-start.11 = (f32[2,32,768]{2,1,0:T(8,128)S(1)}, f32[2,32,768]{2,1,0:T(8,128)S(1)}, u32[]{:S(2)}, u32[]{:S(2)}) collective-permute-start(f32[2,32,768]{2,1,0:T(8,128)S(1)} %pad_maximum_fusion.7), channel_id=1, source_target_pairs={{0,4},{1,5},{2,6},{3,7},{4,0},{5,1},{6,2},{7,3},{8,12},{9,13},{10,... | collective-permute-start | bytes 589832 | tf_op jit(solution)/shard_map/ppermute | solution.py:51
  226.9 7.8 %collective-permute-start.12 = (f32[2,64,768]{2,1,0:T(8,128)S(1)}, f32[2,64,768]{2,1,0:T(8,128)S(1)}, u32[]{:S(2)}, u32[]{:S(2)}) collective-permute-start(f32[2,64,768]{2,1,0:T(8,128)S(1)} %pad_maximum_fusion.2), channel_id=1, source_target_pairs={{0,2},{1,3},{2,0},{3,1},{4,6},{5,7},{6,4},{7,5},{8,10},{9,11},{10,... | collective-permute-start | bytes 1179656 | tf_op jit(solution)/shard_map/ppermute | solution.py:51
  235.7 5.0 %collective-permute-start.13 = (f32[2,128,768]{2,1,0:T(8,128)}, f32[2,128,768]{2,1,0:T(8,128)}, u32[]{:S(2)}, u32[]{:S(2)}) collective-permute-start(f32[2,128,768]{2,1,0:T(8,128)} %pad_maximum_fusion), channel_id=1, source_target_pairs={{0,1},{1,0},{2,3},{3,2},{4,5},{5,4},{6,7},{7,6},{8,9},{9,8},{10,11... | collective-permute-start | bytes 2359304 | tf_op jit(solution)/shard_map/ppermute | solution.py:51
  235.7 67.4 %collective-permute-start.20 = (bf16[256,2048]{1,0:T(8,128)(2,1)}, bf16[256,2048]{1,0:T(8,128)(2,1)}, u32[]{:S(2)}, u32[]{:S(2)}) collective-permute-start(bf16[256,2048]{1,0:T(8,128)(2,1)} %constant_dynamic-slice_fusion.7), channel_id=1, source_target_pairs={{0,16},{16,0},{1,17},{17,1},{2,18},{18,2},{3,19},{19,3},{4,20},{20... | collective-permute-start | bytes 3145736 | tf_op jit(solution)/shard_map/ppermute | solution.py:186
  237.2 72.3 %collective-permute-start.19 = (bf16[256,2048]{1,0:T(8,128)(2,1)}, bf16[256,2048]{1,0:T(8,128)(2,1)S(1)}, u32[]{:S(2)}, u32[]{:S(2)}) collective-permute-start(bf16[256,2048]{1,0:T(8,128)(2,1)} %constant_dynamic-slice_fusion.6), channel_id=1, source_target_pairs={{0,16},{16,0},{1,17},{17,1},{2,18},{18,2},{3,19},{19,3},{4,20},{20... | collective-permute-start | bytes 3145736 | tf_op jit(solution)/shard_map/ppermute | solution.py:186
  237.8 91.7 %collective-permute-start.18 = (bf16[256,4096]{1,0:T(8,128)(2,1)}, bf16[256,4096]{1,0:T(8,128)(2,1)}, u32[]{:S(2)}, u32[]{:S(2)}) collective-permute-start(bf16[256,4096]{1,0:T(8,128)(2,1)} %constant_dynamic-slice_fusion.5), channel_id=1, source_target_pairs={{0,16},{16,0},{1,17},{17,1},{2,18},{18,2},{3,19},{19,3},{4,20},{20... | collective-permute-start | bytes 6291464 | tf_op jit(solution)/shard_map/ppermute | solution.py:186
  239.3 135.2 %collective-permute-start.17 = (bf16[256,4096]{1,0:T(8,128)(2,1)}, bf16[256,4096]{1,0:T(8,128)(2,1)}, u32[]{:S(2)}, u32[]{:S(2)}) collective-permute-start(bf16[256,4096]{1,0:T(8,128)(2,1)} %constant_dynamic-slice_fusion.4), channel_id=1, source_target_pairs={{0,16},{16,0},{1,17},{17,1},{2,18},{18,2},{3,19},{19,3},{4,20},{20... | collective-permute-start | bytes 6291464 | tf_op jit(solution)/shard_map/ppermute | solution.py:186
  240.7 156.2 %collective-permute-start.16 = (bf16[256,2048]{1,0:T(8,128)(2,1)}, bf16[256,2048]{1,0:T(8,128)(2,1)}, u32[]{:S(2)}, u32[]{:S(2)}) collective-permute-start(bf16[256,2048]{1,0:T(8,128)(2,1)} %constant_dynamic-slice_fusion.3), channel_id=1, source_target_pairs={{0,16},{16,0},{1,17},{17,1},{2,18},{18,2},{3,19},{19,3},{4,20},{20... | collective-permute-start | bytes 3145736 | tf_op jit(solution)/shard_map/ppermute | solution.py:186
  303.1 104.9 %collective-permute-start.15 = (bf16[256,1024]{1,0:T(8,128)(2,1)S(1)}, bf16[256,1024]{1,0:T(8,128)(2,1)S(1)}, u32[]{:S(2)}, u32[]{:S(2)}) collective-permute-start(bf16[256,1024]{1,0:T(8,128)(2,1)S(1)} %copy-done.4), channel_id=1, source_target_pairs={{0,16},{16,0},{1,17},{17,1},{2,18},{18,2},{3,19},{19,3},{4,20},{20... | collective-permute-start | bytes 1572872 | tf_op jit(solution)/shard_map/ppermute | solution.py:186
  309.5 104.1 %collective-permute-start.14 = (bf16[256,512]{1,0:T(8,128)(2,1)S(1)}, bf16[256,512]{1,0:T(8,128)(2,1)S(1)}, u32[]{:S(2)}, u32[]{:S(2)}) collective-permute-start(bf16[256,512]{1,0:T(8,128)(2,1)S(1)} %copy-done.7), channel_id=1, source_target_pairs={{0,16},{16,0},{1,17},{17,1},{2,18},{18,2},{3,19},{19,3},{4,20},{20... | collective-permute-start | bytes 786440 | tf_op jit(solution)/shard_map/ppermute | solution.py:186
  311.1 18.4 %copy-start.8 = (bf16[256,512]{1,0:T(8,128)(2,1)S(1)}, bf16[256,512]{1,0:T(8,128)(2,1)}, u32[]{:S(2)}) copy-start(bf16[256,512]{1,0:T(8,128)(2,1)} %constant_dynamic-slice_fusion) | copy-start | bytes 786436
  329.5 89.3 %collective-permute-start = (bf16[256,512]{1,0:T(8,128)(2,1)S(1)}, bf16[256,512]{1,0:T(8,128)(2,1)S(1)}, u32[]{:S(2)}, u32[]{:S(2)}) collective-permute-start(bf16[256,512]{1,0:T(8,128)(2,1)S(1)} %copy-done.8), channel_id=1, source_target_pairs={{0,16},{16,0},{1,17},{17,1},{2,18},{18,2},{3,19},{19,3},{4,20},{20... | collective-permute-start | bytes 786440 | tf_op jit(solution)/shard_map/ppermute | solution.py:186
  (7 other events, 31.8 us)

commit v4 on v3

--- a/solution.py
+++ b/solution.py
@@ -8,10 +8,10 @@
 from jax.sharding import PartitionSpec as P
 
 
-EARLY = (1, 7, 16, 8)
-LATE = (4, 4, 8, 8, 4, 2, 1, 1)
+EARLY = (1, 7, 24)
+LATE = (6, 20, 4, 1, 1)
 UNIT = 64
-BLOCK = 1024
+BLOCKS = (1024, 512, 256, 128)
 
 
 HIGH = lax.Precision.HIGHEST
@@ -248,11 +248,11 @@
     )
     coeffs = coefficients_of(gram, order, rows, features)
 
-    block = min(BLOCK, unit)
     first = jnp.where(me > 0, 0, half)
     out = None
     for start, pieces in ((first, early), (half - first, late)):
         for place, size, got in pieces:
+            block = next(b for b in BLOCKS if size % b == 0 and place % b == 0)
             base = ((start + place) // block).reshape(1).astype(jnp.int32)
             out = update_piece(base, players, slab, got, coeffs, out, size, block)
     return out

time: 425 us -> 416 us (0.979)
  waiting for transfers between devices: 206 us -> 242 us
  Pallas kernels: 97.3 us -> 76.4 us
  local copies, waits for them, and re-layouts: 36.3 us -> 25.4 us
  other arithmetic: 9.52 us -> 2.16 us
    ppermute x12 -> x8, waiting for transfers between devices: 179 us -> 216 us  [send(): return lax.ppermute(piece, 'player', ring[s])]
    pallas_call x12 -> x8, Pallas kernels: 85.5 us -> 64.7 us  [update_piece(): pl.pallas_call(functools.partial(update_kernel, count), out_shape=jax.Sha...]
    dynamic_slice x12 -> x8, local copies, waits for them, and re-layouts: 30.3 us -> 23.8 us  [send(): piece = lax.dynamic_slice(source, (0, start), (rows, size))]
    ppermute x12 -> x8, starting transfers between devices: 14.2 us -> 10.6 us  [send(): return lax.ppermute(piece, 'player', ring[s])]
    dot_general x7 -> x6, matrix products: 43.6 us -> 42.3 us  [dot(): lax.dot_general(a, b, (contract, ((), ())), precision=precision, preferre...]
  transfers between devices with their start and end apart: 21 -> 17, of which waited for: 16 -> 10; matrix products, arithmetic and copies ran while one was open for 18% -> 14% of each run, Pallas kernels for 22% -> 18%
where the time goes in v4:
time: 416 us; the launch traced here: 415 us
  waiting for transfers between devices  242 us (58%)
  Pallas kernels  76.4 us (18%)
  matrix products  42.3 us (10%)
  starting transfers between devices  25.9 us (6%)
  local copies, waits for them, and re-layouts  25.4 us (6%)
    ppermute x8, waiting for transfers between devices, send(): return lax.ppermute(piece, 'player', ring[s])  216 us
    pallas_call x8, Pallas kernels, update_piece(): pl.pallas_call(functools.partial(update_kernel, count), out_shape=jax.Sha...  64.7 us
    dot_general x6, matrix products, dot(): lax.dot_general(a, b, (contract, ((), ())), precision=precision, preferre...  42.3 us
    dynamic_slice x8, local copies, waits for them, and re-layouts, send(): piece = lax.dynamic_slice(source, (0, start), (rows, size))  23.8 us
    ppermute x4, waiting for transfers between devices, scatter_sum(): got = lax.ppermute(send, axis, [(i, i ^ step) for i in range(size)])  11.9 us
    pallas_call x1, Pallas kernels, coefficients_of(): pl.pallas_call(functools.partial(coeff_kernel, rows, features), out_shape...  11.8 us
    ppermute x4, waiting for transfers between devices, gather_back(): got = lax.ppermute(x, axis, [(i, i ^ step) for i in range(size)])  11.5 us
    ppermute x8, starting transfers between devices, send(): return lax.ppermute(piece, 'player', ring[s])  10.6 us
  transfers between devices with their start and end apart: 17, of which 10 were waited for; matrix products, arithmetic and copies ran while one was open for 14% of the time, Pallas kernels for 18%

profile of v4, /device:TPU:0, one launch (start us, length us, event | category | flops | bytes accessed | tf_op | source)
XLA Modules:
  0.0 414.7 jit_solution(16005736610261725954)
XLA Ops:
  1.0 3.0 constant_dynamic-slice_fusion.6
  3.9 3.0 collective-permute-start.2
  6.9 6.1 %constant_dynamic-slice_fusion.5 = bf16[256,12288]{1,0:T(8,128)(2,1)} fusion(bf16[256,32768]{1,0:T(8,128)(2,1)} %w_ref.15, s32[]{:T(128)S(6)} %select_n.176), kind=kLoop, calls=%fused_computation.49 | loop fusion | bytes 12582916 | tf_op jit(solution)/shard_map/dynamic_slice | solution.py:184
  17.8 5.4 %constant_dynamic-slice_fusion.3 = bf16[256,10240]{1,0:T(8,128)(2,1)} fusion(bf16[256,32768]{1,0:T(8,128)(2,1)} %w_ref.15, s32[]{:T(128)S(6)} %select_n.178), kind=kLoop, calls=%fused_computation.47 | loop fusion | bytes 10485764 | tf_op jit(solution)/shard_map/dynamic_slice | solution.py:184
  28.8 12.9 %fusion.10 = f32[256,256]{1,0:T(8,128)S(1)} fusion(bf16[256,32768]{1,0:T(8,128)(2,1)} %w_ref.15), kind=kOutput, calls=%fused_computation.55 | convolution fusion | flops 4294967296 | bytes 17039360 | tf_op jit(solution)/shard_map/dot_general | solution.py:21
  41.8 10.7 %fusion.11 = f32[256,128]{1,0:T(8,128)S(1)} fusion(bf16[256,32768]{1,0:T(8,128)(2,1)} %w_ref.15, bf16[128,32768]{1,0:T(8,128)(2,1)} %x_ref.15), kind=kOutput, calls=%fused_computation.56 | convolution fusion | flops 2147483648 | bytes 25296896 | tf_op jit(solution)/shard_map/dot_general | solution.py:21
  52.5 8.1 %fusion.12 = f32[128,128]{1,0:T(8,128)S(1)} fusion(bf16[128,32768]{1,0:T(8,128)(2,1)} %x_ref.15), kind=kOutput, calls=%fused_computation.57 | convolution fusion | flops 1073741824 | bytes 8454144 | tf_op jit(solution)/shard_map/dot_general | solution.py:21
  64.8 122.9 %collective-permute-done.3.refs_0_ = bf16[256,12288]{1,0:T(8,128)(2,1)} collective-permute-done((bf16[256,12288]{1,0:T(8,128)(2,1)}, bf16[256,12288]{1,0:T(8,128)(2,1)}, u32[]{:S(2)}, u32[]{:S(2)}) %collective-permute-start.3) | collective-permute-done | bytes 6291488 | tf_op jit(solution)/shard_map/ppermute | solution.py:186
  187.7 6.4 %fusion = f32[256,256]{1,0:T(8,128)S(1)} fusion(bf16[256,12288]{1,0:T(8,128)(2,1)} %collective-permute-done.3.refs_0_, bf16[256,32768]{1,0:T(8,128)(2,1)} %w_ref.15, s32[]{:T(128)S(6)} %select_n.192), kind=kOutput, calls=%fused_computation | convolution fusion | flops 1610612736 | bytes 12845060 | tf_op jit(solution)/shard_map/dot_general | solution.py:21
  198.0 5.2 %collective-permute-done.5 = f32[64,768]{1,0:T(8,128)S(1)} collective-permute-done((f32[64,768]{1,0:T(8,128)S(1)}, f32[64,768]{1,0:T(8,128)S(1)}, u32[]{:S(2)}, u32[]{:S(2)}) %collective-permute-start.5) | collective-permute-done | bytes 196640 | tf_op jit(solution)/shard_map/ppermute | solution.py:40
  217.2 2.9 collective-permute-start.9
  220.1 3.1 collective-permute-done.9
  225.6 3.6 collective-permute-done.10
  232.4 4.8 %collective-permute-done.11 = f32[2,64,768]{2,1,0:T(8,128)S(1)} collective-permute-done((f32[2,64,768]{2,1,0:T(8,128)S(1)}, f32[2,64,768]{2,1,0:T(8,128)S(1)}, u32[]{:S(2)}, u32[]{:S(2)}) %collective-permute-start.11) | collective-permute-done | bytes 393248 | tf_op jit(solution)/shard_map/ppermute | solution.py:51
  244.7 11.8 %coefficients_of.1 = (bf16[512,640]{1,0:T(8,128)(2,1)}, bf16[256,640]{1,0:T(8,128)(2,1)}, f32[512,1]{1,0:T(8,128)}, f32[256,1]{1,0:T(8,128)}) custom-call(f32[640,640]{1,0:T(8,128)} %maximum_maximum_fusion.gram_ref, s32[512,1]{1,0:T(8,128)} %copy.30.down_ref, s32[1,512]{1,0:T(1,128)} %bitcast.51), custom_call_target="tpu_custom_call" | custom-call | flops 5033164800 | bytes 3276800 | tf_op jit(solution)/shard_map/coefficients_of/pallas_call | solution.py:95
  256.5 2.9 update_piece.8.refs_5_
  259.5 8.8 %update_piece.9.refs_5_ = bf16[256,32768]{1,0:T(8,128)(2,1)} custom-call(s32[1]{0:T(128)} %bitcast.20.base_ref, bf16[256,32768]{1,0:T(8,128)(2,1)} %w_ref.15, bf16[128,32768]{1,0:T(8,128)(2,1)} %x_ref.15, bf16[256,3584]{1,0:T(8,128)(2,1)} %copy-done, bf16[512,640]{1,0:T(8,128)(2,1)} %get-tuple-element.45.refs_1_, ...), custom_call_target="tpu_custom_call", output_to_operand_aliasing={{}: (8, {})} | custom-call | flops 3523215360 | bytes 6422528 | tf_op jit(solution)/shard_map/update_piece/pallas_call | solution.py:144
  268.3 19.0 %update_piece.10.refs_5_ = bf16[256,32768]{1,0:T(8,128)(2,1)} custom-call(s32[1]{0:T(128)} %bitcast.19.base_ref, bf16[256,32768]{1,0:T(8,128)(2,1)} %w_ref.15, bf16[128,32768]{1,0:T(8,128)(2,1)} %x_ref.15, bf16[256,12288]{1,0:T(8,128)(2,1)} %collective-permute-done.3.refs_0_, ...), custom_call_target="tpu_custom_call", output_to_operand_aliasing={{}: (8, {})} | custom-call | flops 12079595520 | bytes 22020096 | tf_op jit(solution)/shard_map/update_piece/pallas_call | solution.py:144
  287.3 93.5 %collective-permute-done.16.refs_0_ = bf16[256,3072]{1,0:T(8,128)(2,1)} collective-permute-done((bf16[256,3072]{1,0:T(8,128)(2,1)}, bf16[256,3072]{1,0:T(8,128)(2,1)}, u32[]{:S(2)}, u32[]{:S(2)}) %collective-permute-start.16) | collective-permute-done | bytes 1572896 | tf_op jit(solution)/shard_map/ppermute | solution.py:186
  380.8 6.6 %update_piece.11.refs_5_ = bf16[256,32768]{1,0:T(8,128)(2,1)} custom-call(s32[1]{0:T(128)} %bitcast.18.base_ref, bf16[256,32768]{1,0:T(8,128)(2,1)} %w_ref.15, bf16[128,32768]{1,0:T(8,128)(2,1)} %x_ref.15, bf16[256,3072]{1,0:T(8,128)(2,1)} %collective-permute-done.16.refs_0_, ...), custom_call_target="tpu_custom_call", output_to_operand_aliasing={{}: (8, {})} | custom-call | flops 3019898880 | bytes 5505024 | tf_op jit(solution)/shard_map/update_piece/pallas_call | solution.py:144
  387.4 16.3 %update_piece.12.refs_5_ = bf16[256,32768]{1,0:T(8,128)(2,1)} custom-call(s32[1]{0:T(128)} %bitcast.17.base_ref, bf16[256,32768]{1,0:T(8,128)(2,1)} %w_ref.15, bf16[128,32768]{1,0:T(8,128)(2,1)} %x_ref.15, bf16[256,10240]{1,0:T(8,128)(2,1)} %collective-permute-done.15.refs_0_, ...), custom_call_target="tpu_custom_call", output_to_operand_aliasing={{}: (8, {})} | custom-call | flops 10066329600 | bytes 18350080 | tf_op jit(solution)/shard_map/update_piece/pallas_call | solution.py:144
  403.6 5.2 %update_piece.13.refs_5_ = bf16[256,32768]{1,0:T(8,128)(2,1)} custom-call(s32[1]{0:T(128)} %bitcast.16.base_ref, bf16[256,32768]{1,0:T(8,128)(2,1)} %w_ref.15, bf16[128,32768]{1,0:T(8,128)(2,1)} %x_ref.15, bf16[256,2048]{1,0:T(8,128)(2,1)} %collective-permute-done.14.refs_0_, ...), custom_call_target="tpu_custom_call", output_to_operand_aliasing={{}: (8, {})} | custom-call | flops 2013265920 | bytes 3670016 | tf_op jit(solution)/shard_map/update_piece/pallas_call | solution.py:144
  408.8 2.9 update_piece.14.refs_5_
  411.7 2.9 update_piece.15
  (74 shorter events, 46.3 us)
Async XLA Ops:
  3.9 58.0 %collective-permute-start.2 = (bf16[256,3584]{1,0:T(8,128)(2,1)}, bf16[256,3584]{1,0:T(8,128)(2,1)S(1)}, u32[]{:S(2)}, u32[]{:S(2)}) collective-permute-start(bf16[256,3584]{1,0:T(8,128)(2,1)} %constant_dynamic-slice_fusion.6), channel_id=1, source_target_pairs={{0,16},{16,0},{1,17},{17,1},{2,18},{18,2},{3,19},{19,3},{4,20},{20... | collective-permute-start | bytes 5505032 | tf_op jit(solution)/shard_map/ppermute | solution.py:186
  6.9 53.7 %collective-permute-start.1 = (bf16[256,512]{1,0:T(8,128)(2,1)S(1)}, bf16[256,512]{1,0:T(8,128)(2,1)S(1)}, u32[]{:S(2)}, u32[]{:S(2)}) collective-permute-start(bf16[256,512]{1,0:T(8,128)(2,1)S(1)} %constant_dynamic-slice_fusion.7), channel_id=1, source_target_pairs={{0,16},{16,0},{1,17},{17,1},{2,18},{18,2},{3,19},{19,3},{4,20},{20... | collective-permute-start | bytes 786440 | tf_op jit(solution)/shard_map/ppermute | solution.py:186
  13.1 174.6 %collective-permute-start.3 = (bf16[256,12288]{1,0:T(8,128)(2,1)}, bf16[256,12288]{1,0:T(8,128)(2,1)}, u32[]{:S(2)}, u32[]{:S(2)}) collective-permute-start(bf16[256,12288]{1,0:T(8,128)(2,1)} %constant_dynamic-slice_fusion.5), channel_id=1, source_target_pairs={{0,16},{16,0},{1,17},{17,1},{2,18},{18,2},{3,19},{19,3},{4,20},{20... | collective-permute-start | bytes 18874376 | tf_op jit(solution)/shard_map/ppermute | solution.py:186
  60.6 133.5 %copy-start.1 = (bf16[256,512]{1,0:T(8,128)(2,1)}, bf16[256,512]{1,0:T(8,128)(2,1)S(1)}, u32[]{:S(2)}) copy-start(bf16[256,512]{1,0:T(8,128)(2,1)S(1)} %collective-permute-done.1.refs_0_) | copy-start | bytes 786436
  61.9 132.2 %copy-start = (bf16[256,3584]{1,0:T(8,128)(2,1)}, bf16[256,3584]{1,0:T(8,128)(2,1)S(1)}, u32[]{:S(2)}) copy-start(bf16[256,3584]{1,0:T(8,128)(2,1)S(1)} %collective-permute-done.2.refs_0_) | copy-start | bytes 5505028
  194.3 1.8 collective-permute-start.4
  196.2 7.0 %collective-permute-start.5 = (f32[64,768]{1,0:T(8,128)S(1)}, f32[64,768]{1,0:T(8,128)S(1)}, u32[]{:S(2)}, u32[]{:S(2)}) collective-permute-start(f32[64,768]{1,0:T(8,128)S(1)} %slice_select_fusion.1), channel_id=1, source_target_pairs={{0,2},{1,3},{2,0},{3,1},{4,6},{5,7},{6,4},{7,5},{8,10},{9,11},{10,... | collective-permute-start | bytes 589832 | tf_op jit(solution)/shard_map/ppermute | solution.py:40
  203.3 4.7 %collective-permute-start.6 = (f32[32,768]{1,0:T(8,128)S(1)}, f32[32,768]{1,0:T(8,128)S(1)}, u32[]{:S(2)}, u32[]{:S(2)}) collective-permute-start(f32[32,768]{1,0:T(8,128)S(1)} %slice_select_fusion.2), channel_id=1, source_target_pairs={{0,4},{1,5},{2,6},{3,7},{4,0},{5,1},{6,2},{7,3},{8,12},{9,13},{10,... | collective-permute-start | bytes 294920 | tf_op jit(solution)/shard_map/ppermute | solution.py:40
  208.0 5.1 %collective-permute-start.7 = (f32[16,768]{1,0:T(8,128)S(1)}, f32[16,768]{1,0:T(8,128)S(1)}, u32[]{:S(2)}, u32[]{:S(2)}) collective-permute-start(f32[16,768]{1,0:T(8,128)S(1)} %slice_select_fusion.3), channel_id=1, source_target_pairs={{0,8},{1,9},{2,10},{3,11},{4,12},{5,13},{6,14},{7,15},{8,0},{9,1},... | collective-permute-start | bytes 147464 | tf_op jit(solution)/shard_map/ppermute | solution.py:40
  213.1 4.2 %collective-permute-start.8 = (f32[16,768]{1,0:T(8,128)S(1)}, f32[16,768]{1,0:T(8,128)S(1)}, u32[]{:S(2)}, u32[]{:S(2)}) collective-permute-start(f32[16,768]{1,0:T(8,128)S(1)} %select_add_fusion.3), channel_id=1, source_target_pairs={{0,16},{16,0},{1,17},{17,1},{2,18},{18,2},{3,19},{19,3},{4,20},{20... | collective-permute-start | bytes 147464 | tf_op jit(solution)/shard_map/ppermute | solution.py:226
  217.2 6.0 %collective-permute-start.9 = (f32[2,16,768]{2,1,0:T(8,128)S(1)}, f32[2,16,768]{2,1,0:T(8,128)S(1)}, u32[]{:S(2)}, u32[]{:S(2)}) collective-permute-start(f32[2,16,768]{2,1,0:T(8,128)S(1)} %pad_maximum_fusion.10), channel_id=1, source_target_pairs={{0,8},{1,9},{2,10},{3,11},{4,12},{5,13},{6,14},{7,15},{8,0},{9,1},... | collective-permute-start | bytes 294920 | tf_op jit(solution)/shard_map/ppermute | solution.py:51
  223.3 6.0 %collective-permute-start.10 = (f32[2,32,768]{2,1,0:T(8,128)S(1)}, f32[2,32,768]{2,1,0:T(8,128)S(1)}, u32[]{:S(2)}, u32[]{:S(2)}) collective-permute-start(f32[2,32,768]{2,1,0:T(8,128)S(1)} %pad_maximum_fusion.7), channel_id=1, source_target_pairs={{0,4},{1,5},{2,6},{3,7},{4,0},{5,1},{6,2},{7,3},{8,12},{9,13},{10,... | collective-permute-start | bytes 589832 | tf_op jit(solution)/shard_map/ppermute | solution.py:51
  229.3 7.8 %collective-permute-start.11 = (f32[2,64,768]{2,1,0:T(8,128)S(1)}, f32[2,64,768]{2,1,0:T(8,128)S(1)}, u32[]{:S(2)}, u32[]{:S(2)}) collective-permute-start(f32[2,64,768]{2,1,0:T(8,128)S(1)} %pad_maximum_fusion.2), channel_id=1, source_target_pairs={{0,2},{1,3},{2,0},{3,1},{4,6},{5,7},{6,4},{7,5},{8,10},{9,11},{10,... | collective-permute-start | bytes 1179656 | tf_op jit(solution)/shard_map/ppermute | solution.py:51
  230.9 156.5 %collective-permute-start.15 = (bf16[256,10240]{1,0:T(8,128)(2,1)}, bf16[256,10240]{1,0:T(8,128)(2,1)}, u32[]{:S(2)}, u32[]{:S(2)}) collective-permute-start(bf16[256,10240]{1,0:T(8,128)(2,1)} %constant_dynamic-slice_fusion.3), channel_id=1, source_target_pairs={{0,16},{16,0},{1,17},{17,1},{2,18},{18,2},{3,19},{19,3},{4,20},{20... | collective-permute-start | bytes 15728648 | tf_op jit(solution)/shard_map/ppermute | solution.py:186
  237.3 4.6 %collective-permute-start.12 = (f32[2,128,768]{2,1,0:T(8,128)S(1)}, f32[2,128,768]{2,1,0:T(8,128)S(1)}, u32[]{:S(2)}, u32[]{:S(2)}) collective-permute-start(f32[2,128,768]{2,1,0:T(8,128)S(1)} %pad_maximum_fusion), channel_id=1, source_target_pairs={{0,1},{1,0},{2,3},{3,2},{4,5},{5,4},{6,7},{7,6},{8,9},{9,8},{10,11... | collective-permute-start | bytes 2359304 | tf_op jit(solution)/shard_map/ppermute | solution.py:51
  237.3 143.5 %collective-permute-start.16 = (bf16[256,3072]{1,0:T(8,128)(2,1)}, bf16[256,3072]{1,0:T(8,128)(2,1)}, u32[]{:S(2)}, u32[]{:S(2)}) collective-permute-start(bf16[256,3072]{1,0:T(8,128)(2,1)} %constant_dynamic-slice_fusion.4), channel_id=1, source_target_pairs={{0,16},{16,0},{1,17},{17,1},{2,18},{18,2},{3,19},{19,3},{4,20},{20... | collective-permute-start | bytes 4718600 | tf_op jit(solution)/shard_map/ppermute | solution.py:186
  238.9 164.7 %collective-permute-start.14 = (bf16[256,2048]{1,0:T(8,128)(2,1)}, bf16[256,2048]{1,0:T(8,128)(2,1)}, u32[]{:S(2)}, u32[]{:S(2)}) collective-permute-start(bf16[256,2048]{1,0:T(8,128)(2,1)} %constant_dynamic-slice_fusion.2), channel_id=1, source_target_pairs={{0,16},{16,0},{1,17},{17,1},{2,18},{18,2},{3,19},{19,3},{4,20},{20... | collective-permute-start | bytes 3145736 | tf_op jit(solution)/shard_map/ppermute | solution.py:186
  239.4 169.4 %collective-permute-start.13 = (bf16[256,512]{1,0:T(8,128)(2,1)}, bf16[256,512]{1,0:T(8,128)(2,1)}, u32[]{:S(2)}, u32[]{:S(2)}) collective-permute-start(bf16[256,512]{1,0:T(8,128)(2,1)} %constant_dynamic-slice_fusion.1), channel_id=1, source_target_pairs={{0,16},{16,0},{1,17},{17,1},{2,18},{18,2},{3,19},{19,3},{4,20},{20... | collective-permute-start | bytes 786440 | tf_op jit(solution)/shard_map/ppermute | solution.py:186
  241.0 3.8 copy-start.2
  241.8 169.9 %collective-permute-start = (bf16[256,512]{1,0:T(8,128)(2,1)}, bf16[256,512]{1,0:T(8,128)(2,1)}, u32[]{:S(2)}, u32[]{:S(2)}) collective-permute-start(bf16[256,512]{1,0:T(8,128)(2,1)} %constant_dynamic-slice_fusion), channel_id=1, source_target_pairs={{0,16},{16,0},{1,17},{17,1},{2,18},{18,2},{3,19},{19,3},{4,20},{20... | collective-permute-start | bytes 786440 | tf_op jit(solution)/shard_map/ppermute | solution.py:186

commit v5 on v4

--- a/solution.py
+++ b/solution.py
@@ -10,6 +10,7 @@
 
 EARLY = (1, 7, 24)
 LATE = (6, 20, 4, 1, 1)
+NEAR = 1
 UNIT = 64
 BLOCKS = (1024, 512, 256, 128)
 
@@ -126,15 +127,21 @@
     out_ref[...] = (dot(j1_ref[...], scaled[...]) * d1_ref[...]).astype(jnp.bfloat16)
 
 
-def update_piece(base, weights, slab, others, coeffs, out, width, block):
+def update_piece(base, weights, slab, others, coeffs, out, width, block, near):
     rows, batch = weights.shape[0], slab.shape[0]
     count = len(others)
     shift = lambda i, b: (0, b[0] + i)
-    whole = lambda i, b: (0, 0)
     in_specs = [pl.BlockSpec((rows, block), shift), pl.BlockSpec((batch, block), shift)]
     in_specs += [pl.BlockSpec((rows, block), lambda i, b: (0, i))] * count
-    in_specs += [pl.BlockSpec(c.shape, whole) for c in coeffs]
-    operands = [weights, slab, *others, *coeffs]
+    if near:
+        cut = lambda x: lax.dynamic_slice(x, (0, base[0] * block), (x.shape[0], block))
+        inputs = [cut(weights), cut(slab), *others]
+        inputs = [pltpu.with_memory_space_constraint(x, pltpu.VMEM) for x in inputs]
+        in_specs = [pl.BlockSpec(memory_space=pltpu.VMEM)] * len(inputs)
+    else:
+        inputs = [weights, slab, *others]
+    in_specs += [pl.BlockSpec(memory_space=pltpu.VMEM)] * len(coeffs)
+    operands = [*inputs, *coeffs]
     aliases = {}
     if out is not None:
         in_specs.append(pl.BlockSpec(memory_space=pl.ANY))
@@ -247,14 +254,16 @@
         [((me - t) % n) * rows + jnp.arange(rows, dtype=jnp.int32) for t in turn]
     )
     coeffs = coefficients_of(gram, order, rows, features)
+    coeffs = [pltpu.with_memory_space_constraint(c, pltpu.VMEM) for c in coeffs]
 
     first = jnp.where(me > 0, 0, half)
     out = None
-    for start, pieces in ((first, early), (half - first, late)):
-        for place, size, got in pieces:
+    for name, start, pieces in (("e", first, early), ("l", half - first, late)):
+        for k, (place, size, got) in enumerate(pieces):
             block = next(b for b in BLOCKS if size % b == 0 and place % b == 0)
             base = ((start + place) // block).reshape(1).astype(jnp.int32)
-            out = update_piece(base, players, slab, got, coeffs, out, size, block)
+            near = name == "l" and size == block and k >= len(LATE) - NEAR
+            out = update_piece(base, players, slab, got, coeffs, out, size, block, near)
     return out
 
 

time: 416 us -> 423 us (1.017)
  local copies, waits for them, and re-layouts: 25.4 us -> 32.6 us
  Pallas kernels: 76.4 us -> 71.7 us
  other arithmetic: 2.16 us -> 6.82 us
    unnamed x10 -> x20, local copies, waits for them, and re-layouts: 0.46 us -> 6.61 us
    pallas_call x8, Pallas kernels: 64.7 us -> 59.9 us  [update_piece(): pl.pallas_call(functools.partial(update_kernel, count), out_shape=jax.Sha...]
  transfers between devices with their start and end apart: 17 -> 17, of which waited for: 10 -> 10; matrix products, arithmetic and copies ran while one was open for 14% -> 14% of each run, Pallas kernels for 18% -> 17%
where the time goes in v5:
time: 423 us; the launch traced here: 422 us
  waiting for transfers between devices  242 us (57%)
  Pallas kernels  71.7 us (17%)
  matrix products  42.3 us (10%)
  local copies, waits for them, and re-layouts  32.6 us (8%)
  starting transfers between devices  25.9 us (6%)
  other arithmetic  6.82 us (2%)
    ppermute x8, waiting for transfers between devices, send(): return lax.ppermute(piece, 'player', ring[s])  216 us
    pallas_call x8, Pallas kernels, update_piece(): pl.pallas_call(functools.partial(update_kernel, count), out_shape=jax.Sha...  59.9 us
    dot_general x6, matrix products, dot(): lax.dot_general(a, b, (contract, ((), ())), precision=precision, preferre...  42.3 us
    dynamic_slice x8, local copies, waits for them, and re-layouts, send(): piece = lax.dynamic_slice(source, (0, start), (rows, size))  23.9 us
    ppermute x4, waiting for transfers between devices, scatter_sum(): got = lax.ppermute(send, axis, [(i, i ^ step) for i in range(size)])  11.9 us
    pallas_call x1, Pallas kernels, coefficients_of(): pl.pallas_call(functools.partial(coeff_kernel, rows, features), out_shape...  11.8 us
    ppermute x4, waiting for transfers between devices, gather_back(): got = lax.ppermute(x, axis, [(i, i ^ step) for i in range(size)])  11.5 us
    ppermute x8, starting transfers between devices, send(): return lax.ppermute(piece, 'player', ring[s])  10.6 us
  transfers between devices with their start and end apart: 17, of which 10 were waited for; matrix products, arithmetic and copies ran while one was open for 14% of the time, Pallas kernels for 17%

profile of v5, /device:TPU:0, one launch (start us, length us, event | category | flops | bytes accessed | tf_op | source)
XLA Modules:
  0.0 421.7 jit_solution(14650974267927157890)
XLA Ops:
  1.1 3.0 constant_dynamic-slice_fusion.6
  4.0 6.1 %constant_dynamic-slice_fusion.5 = bf16[256,12288]{1,0:T(8,128)(2,1)} fusion(bf16[256,32768]{1,0:T(8,128)(2,1)} %w_ref.13, s32[]{:T(128)S(6)} %select_n.181), kind=kLoop, calls=%fused_computation.49 | loop fusion | bytes 12582916 | tf_op jit(solution)/shard_map/dynamic_slice | solution.py:191
  10.2 3.0 collective-permute-start.3
  17.8 5.4 %constant_dynamic-slice_fusion.3 = bf16[256,10240]{1,0:T(8,128)(2,1)} fusion(bf16[256,32768]{1,0:T(8,128)(2,1)} %w_ref.13, s32[]{:T(128)S(6)} %select_n.183), kind=kLoop, calls=%fused_computation.47 | loop fusion | bytes 10485764 | tf_op jit(solution)/shard_map/dynamic_slice | solution.py:191
  28.9 12.9 %fusion.10 = f32[256,256]{1,0:T(8,128)S(1)} fusion(bf16[256,32768]{1,0:T(8,128)(2,1)} %w_ref.13), kind=kOutput, calls=%fused_computation.57 | convolution fusion | flops 4294967296 | bytes 17039360 | tf_op jit(solution)/shard_map/dot_general | solution.py:22
  41.9 10.7 %fusion.11 = f32[256,128]{1,0:T(8,128)S(1)} fusion(bf16[256,32768]{1,0:T(8,128)(2,1)} %w_ref.13, bf16[128,32768]{1,0:T(8,128)(2,1)} %x_ref.13), kind=kOutput, calls=%fused_computation.58 | convolution fusion | flops 2147483648 | bytes 25296896 | tf_op jit(solution)/shard_map/dot_general | solution.py:22
  52.6 8.1 %fusion.12 = f32[128,128]{1,0:T(8,128)S(1)} fusion(bf16[128,32768]{1,0:T(8,128)(2,1)} %x_ref.13), kind=kOutput, calls=%fused_computation.59 | convolution fusion | flops 1073741824 | bytes 8454144 | tf_op jit(solution)/shard_map/dot_general | solution.py:22
  60.7 133.1 %collective-permute-done.1.refs_0_ = bf16[256,512]{1,0:T(8,128)(2,1)S(1)} collective-permute-done((bf16[256,512]{1,0:T(8,128)(2,1)S(1)}, bf16[256,512]{1,0:T(8,128)(2,1)S(1)}, u32[]{:S(2)}, u32[]{:S(2)}) %collective-permute-start.1) | collective-permute-done | bytes 262176 | tf_op jit(solution)/shard_map/ppermute | solution.py:193
  195.1 2.8 fusion.2
  198.0 6.4 %fusion = f32[256,256]{1,0:T(8,128)S(1)} fusion(bf16[256,12288]{1,0:T(8,128)(2,1)} %collective-permute-done.3.refs_0_, bf16[256,32768]{1,0:T(8,128)(2,1)} %w_ref.13, s32[]{:T(128)S(6)} %select_n.197), kind=kOutput, calls=%fused_computation | convolution fusion | flops 1610612736 | bytes 12845060 | tf_op jit(solution)/shard_map/dot_general | solution.py:22
  208.4 5.2 %collective-permute-done.5 = f32[64,768]{1,0:T(8,128)S(1)} collective-permute-done((f32[64,768]{1,0:T(8,128)S(1)}, f32[64,768]{1,0:T(8,128)S(1)}, u32[]{:S(2)}, u32[]{:S(2)}) %collective-permute-start.5) | collective-permute-done | bytes 196640 | tf_op jit(solution)/shard_map/ppermute | solution.py:41
  215.5 2.8 collective-permute-done.6
  218.3 2.9 collective-permute-start.7
  227.6 2.9 collective-permute-start.9
  230.5 3.1 collective-permute-done.9
  235.9 3.6 collective-permute-done.10
  242.7 4.8 %collective-permute-done.11 = f32[2,64,768]{2,1,0:T(8,128)S(1)} collective-permute-done((f32[2,64,768]{2,1,0:T(8,128)S(1)}, f32[2,64,768]{2,1,0:T(8,128)S(1)}, u32[]{:S(2)}, u32[]{:S(2)}) %collective-permute-start.11) | collective-permute-done | bytes 393248 | tf_op jit(solution)/shard_map/ppermute | solution.py:52
  262.9 11.8 %coefficients_of.1 = (bf16[512,640]{1,0:T(8,128)(2,1)}, bf16[256,640]{1,0:T(8,128)(2,1)}, f32[512,1]{1,0:T(8,128)}, f32[256,1]{1,0:T(8,128)}) custom-call(f32[640,640]{1,0:T(8,128)} %maximum_maximum_fusion.gram_ref, s32[512,1]{1,0:T(8,128)} %copy.30.down_ref, s32[1,512]{1,0:T(1,128)} %bitcast.51), custom_call_target="tpu_custom_call" | custom-call | flops 5033164800 | bytes 3276800 | tf_op jit(solution)/shard_map/coefficients_of/pallas_call | solution.py:96
  281.1 8.4 %update_piece.9.refs_5_ = bf16[256,32768]{1,0:T(8,128)(2,1)} custom-call(s32[1]{0:T(128)} %bitcast.20.base_ref, bf16[256,32768]{1,0:T(8,128)(2,1)} %w_ref.13, bf16[128,32768]{1,0:T(8,128)(2,1)} %x_ref.13, bf16[256,3584]{1,0:T(8,128)(2,1)} %copy-done.4, bf16[512,640]{1,0:T(8,128)(2,1)S(1)} %copy-done, ...), custom_call_target="tpu_custom_call", output_to_operand_aliasing={{}: (8, {})} | custom-call | flops 3523215360 | bytes 6422528 | tf_op jit(solution)/shard_map/update_piece/pallas_call | solution.py:151
  289.5 18.5 %update_piece.10.refs_5_ = bf16[256,32768]{1,0:T(8,128)(2,1)} custom-call(s32[1]{0:T(128)} %bitcast.19.base_ref, bf16[256,32768]{1,0:T(8,128)(2,1)} %w_ref.13, bf16[128,32768]{1,0:T(8,128)(2,1)} %x_ref.13, bf16[256,12288]{1,0:T(8,128)(2,1)} %collective-permute-done.3.refs_0_, bf16[512,640]{1,0:T(8,128)(2,1)S(1)} %copy-done, ...), custom_call_target="tpu_custom_call", output_to_operand_aliasing={{}: (8, {})} | custom-call | flops 12079595520 | bytes 22020096 | tf_op jit(solution)/shard_map/update_piece/pallas_call | solution.py:151
  308.0 83.1 %collective-permute-done.16.refs_0_ = bf16[256,3072]{1,0:T(8,128)(2,1)} collective-permute-done((bf16[256,3072]{1,0:T(8,128)(2,1)}, bf16[256,3072]{1,0:T(8,128)(2,1)}, u32[]{:S(2)}, u32[]{:S(2)}) %collective-permute-start.16) | collective-permute-done | bytes 1572896 | tf_op jit(solution)/shard_map/ppermute | solution.py:193
  391.2 6.1 %update_piece.11.refs_5_ = bf16[256,32768]{1,0:T(8,128)(2,1)} custom-call(s32[1]{0:T(128)} %bitcast.18.base_ref, bf16[256,32768]{1,0:T(8,128)(2,1)} %w_ref.13, bf16[128,32768]{1,0:T(8,128)(2,1)} %x_ref.13, bf16[256,3072]{1,0:T(8,128)(2,1)} %collective-permute-done.16.refs_0_, bf16[512,640]{1,0:T(8,128)(2,1)S(1)} %copy-done, ...), custom_call_target="tpu_custom_call", output_to_operand_aliasing={{}: (8, {})} | custom-call | flops 3019898880 | bytes 5505024 | tf_op jit(solution)/shard_map/update_piece/pallas_call | solution.py:151
  397.3 15.8 %update_piece.12.refs_5_ = bf16[256,32768]{1,0:T(8,128)(2,1)} custom-call(s32[1]{0:T(128)} %bitcast.17.base_ref, bf16[256,32768]{1,0:T(8,128)(2,1)} %w_ref.13, bf16[128,32768]{1,0:T(8,128)(2,1)} %x_ref.13, bf16[256,10240]{1,0:T(8,128)(2,1)} %collective-permute-done.15.refs_0_, bf16[512,640]{1,0:T(8,128)(2,1)S(1)} %copy-done, ...), custom_call_target="tpu_custom_call", output_to_operand_aliasing={{}: (8, {})} | custom-call | flops 10066329600 | bytes 18350080 | tf_op jit(solution)/shard_map/update_piece/pallas_call | solution.py:151
  413.0 4.7 %update_piece.13.refs_5_ = bf16[256,32768]{1,0:T(8,128)(2,1)} custom-call(s32[1]{0:T(128)} %bitcast.16.base_ref, bf16[256,32768]{1,0:T(8,128)(2,1)} %w_ref.13, bf16[128,32768]{1,0:T(8,128)(2,1)} %x_ref.13, bf16[256,2048]{1,0:T(8,128)(2,1)} %collective-permute-done.14.refs_0_, bf16[512,640]{1,0:T(8,128)(2,1)S(1)} %copy-done, ...), custom_call_target="tpu_custom_call", output_to_operand_aliasing={{}: (8, {})} | custom-call | flops 2013265920 | bytes 3670016 | tf_op jit(solution)/shard_map/update_piece/pallas_call | solution.py:151
  (85 shorter events, 56.1 us)
Async XLA Ops:
  10.2 187.9 %collective-permute-start.3 = (bf16[256,12288]{1,0:T(8,128)(2,1)}, bf16[256,12288]{1,0:T(8,128)(2,1)}, u32[]{:S(2)}, u32[]{:S(2)}) collective-permute-start(bf16[256,12288]{1,0:T(8,128)(2,1)} %constant_dynamic-slice_fusion.5), channel_id=1, source_target_pairs={{0,16},{16,0},{1,17},{17,1},{2,18},{18,2},{3,19},{19,3},{4,20},{20... | collective-permute-start | bytes 18874376 | tf_op jit(solution)/shard_map/ppermute | solution.py:193
  13.1 182.0 %collective-permute-start.2 = (bf16[256,3584]{1,0:T(8,128)(2,1)}, bf16[256,3584]{1,0:T(8,128)(2,1)S(1)}, u32[]{:S(2)}, u32[]{:S(2)}) collective-permute-start(bf16[256,3584]{1,0:T(8,128)(2,1)} %constant_dynamic-slice_fusion.6), channel_id=1, source_target_pairs={{0,16},{16,0},{1,17},{17,1},{2,18},{18,2},{3,19},{19,3},{4,20},{20... | collective-permute-start | bytes 5505032 | tf_op jit(solution)/shard_map/ppermute | solution.py:193
  13.2 180.6 %collective-permute-start.1 = (bf16[256,512]{1,0:T(8,128)(2,1)S(1)}, bf16[256,512]{1,0:T(8,128)(2,1)S(1)}, u32[]{:S(2)}, u32[]{:S(2)}) collective-permute-start(bf16[256,512]{1,0:T(8,128)(2,1)S(1)} %get-tuple-element.38), channel_id=1, source_target_pairs={{0,16},{16,0},{1,17},{17,1},{2,18},{18,2},{3,19},{19,3},{4,20},{20... | collective-permute-start | bytes 786440 | tf_op jit(solution)/shard_map/ppermute | solution.py:193
  193.8 10.7 %copy-start.5 = (bf16[256,512]{1,0:T(8,128)(2,1)}, bf16[256,512]{1,0:T(8,128)(2,1)S(1)}, u32[]{:S(2)}) copy-start(bf16[256,512]{1,0:T(8,128)(2,1)S(1)} %collective-permute-done.1.refs_0_) | copy-start | bytes 786436
  195.1 9.4 %copy-start.4 = (bf16[256,3584]{1,0:T(8,128)(2,1)}, bf16[256,3584]{1,0:T(8,128)(2,1)S(1)}, u32[]{:S(2)}) copy-start(bf16[256,3584]{1,0:T(8,128)(2,1)S(1)} %collective-permute-done.2.refs_0_) | copy-start | bytes 5505028
  204.7 1.8 collective-permute-start.4
  206.5 7.0 %collective-permute-start.5 = (f32[64,768]{1,0:T(8,128)S(1)}, f32[64,768]{1,0:T(8,128)S(1)}, u32[]{:S(2)}, u32[]{:S(2)}) collective-permute-start(f32[64,768]{1,0:T(8,128)S(1)} %slice_select_fusion.1), channel_id=1, source_target_pairs={{0,2},{1,3},{2,0},{3,1},{4,6},{5,7},{6,4},{7,5},{8,10},{9,11},{10,... | collective-permute-start | bytes 589832 | tf_op jit(solution)/shard_map/ppermute | solution.py:41
  213.6 4.7 %collective-permute-start.6 = (f32[32,768]{1,0:T(8,128)S(1)}, f32[32,768]{1,0:T(8,128)S(1)}, u32[]{:S(2)}, u32[]{:S(2)}) collective-permute-start(f32[32,768]{1,0:T(8,128)S(1)} %slice_select_fusion.2), channel_id=1, source_target_pairs={{0,4},{1,5},{2,6},{3,7},{4,0},{5,1},{6,2},{7,3},{8,12},{9,13},{10,... | collective-permute-start | bytes 294920 | tf_op jit(solution)/shard_map/ppermute | solution.py:41
  218.3 5.1 %collective-permute-start.7 = (f32[16,768]{1,0:T(8,128)S(1)}, f32[16,768]{1,0:T(8,128)S(1)}, u32[]{:S(2)}, u32[]{:S(2)}) collective-permute-start(f32[16,768]{1,0:T(8,128)S(1)} %slice_select_fusion.3), channel_id=1, source_target_pairs={{0,8},{1,9},{2,10},{3,11},{4,12},{5,13},{6,14},{7,15},{8,0},{9,1},... | collective-permute-start | bytes 147464 | tf_op jit(solution)/shard_map/ppermute | solution.py:41
  223.4 4.2 collective-permute-start.8
  227.6 6.0 %collective-permute-start.9 = (f32[2,16,768]{2,1,0:T(8,128)S(1)}, f32[2,16,768]{2,1,0:T(8,128)S(1)}, u32[]{:S(2)}, u32[]{:S(2)}) collective-permute-start(f32[2,16,768]{2,1,0:T(8,128)S(1)} %pad_maximum_fusion.10), channel_id=1, source_target_pairs={{0,8},{1,9},{2,10},{3,11},{4,12},{5,13},{6,14},{7,15},{8,0},{9,1},... | collective-permute-start | bytes 294920 | tf_op jit(solution)/shard_map/ppermute | solution.py:52
  233.6 6.0 %collective-permute-start.10 = (f32[2,32,768]{2,1,0:T(8,128)S(1)}, f32[2,32,768]{2,1,0:T(8,128)S(1)}, u32[]{:S(2)}, u32[]{:S(2)}) collective-permute-start(f32[2,32,768]{2,1,0:T(8,128)S(1)} %pad_maximum_fusion.7), channel_id=1, source_target_pairs={{0,4},{1,5},{2,6},{3,7},{4,0},{5,1},{6,2},{7,3},{8,12},{9,13},{10,... | collective-permute-start | bytes 589832 | tf_op jit(solution)/shard_map/ppermute | solution.py:52
  239.7 7.8 %collective-permute-start.11 = (f32[2,64,768]{2,1,0:T(8,128)S(1)}, f32[2,64,768]{2,1,0:T(8,128)S(1)}, u32[]{:S(2)}, u32[]{:S(2)}) collective-permute-start(f32[2,64,768]{2,1,0:T(8,128)S(1)} %pad_maximum_fusion.2), channel_id=1, source_target_pairs={{0,2},{1,3},{2,0},{3,1},{4,6},{5,7},{6,4},{7,5},{8,10},{9,11},{10,... | collective-permute-start | bytes 1179656 | tf_op jit(solution)/shard_map/ppermute | solution.py:52
  241.2 156.0 %collective-permute-start.15 = (bf16[256,10240]{1,0:T(8,128)(2,1)}, bf16[256,10240]{1,0:T(8,128)(2,1)}, u32[]{:S(2)}, u32[]{:S(2)}) collective-permute-start(bf16[256,10240]{1,0:T(8,128)(2,1)} %constant_dynamic-slice_fusion.3), channel_id=1, source_target_pairs={{0,16},{16,0},{1,17},{17,1},{2,18},{18,2},{3,19},{19,3},{4,20},{20... | collective-permute-start | bytes 15728648 | tf_op jit(solution)/shard_map/ppermute | solution.py:193
  247.6 5.5 %collective-permute-start.12 = (f32[2,128,768]{2,1,0:T(8,128)S(1)}, f32[2,128,768]{2,1,0:T(8,128)S(1)}, u32[]{:S(2)}, u32[]{:S(2)}) collective-permute-start(f32[2,128,768]{2,1,0:T(8,128)S(1)} %pad_maximum_fusion), channel_id=1, source_target_pairs={{0,1},{1,0},{2,3},{3,2},{4,5},{5,4},{6,7},{7,6},{8,9},{9,8},{10,11... | collective-permute-start | bytes 2359304 | tf_op jit(solution)/shard_map/ppermute | solution.py:52
  247.7 143.5 %collective-permute-start.16 = (bf16[256,3072]{1,0:T(8,128)(2,1)}, bf16[256,3072]{1,0:T(8,128)(2,1)}, u32[]{:S(2)}, u32[]{:S(2)}) collective-permute-start(bf16[256,3072]{1,0:T(8,128)(2,1)} %constant_dynamic-slice_fusion.4), channel_id=1, source_target_pairs={{0,16},{16,0},{1,17},{17,1},{2,18},{18,2},{3,19},{19,3},{4,20},{20... | collective-permute-start | bytes 4718600 | tf_op jit(solution)/shard_map/ppermute | solution.py:193
  249.3 163.8 %collective-permute-start.14 = (bf16[256,2048]{1,0:T(8,128)(2,1)}, bf16[256,2048]{1,0:T(8,128)(2,1)}, u32[]{:S(2)}, u32[]{:S(2)}) collective-permute-start(bf16[256,2048]{1,0:T(8,128)(2,1)} %constant_dynamic-slice_fusion.2), channel_id=1, source_target_pairs={{0,16},{16,0},{1,17},{17,1},{2,18},{18,2},{3,19},{19,3},{4,20},{20... | collective-permute-start | bytes 3145736 | tf_op jit(solution)/shard_map/ppermute | solution.py:193
  249.8 167.9 %collective-permute-start.13 = (bf16[256,512]{1,0:T(8,128)(2,1)}, bf16[256,512]{1,0:T(8,128)(2,1)}, u32[]{:S(2)}, u32[]{:S(2)}) collective-permute-start(bf16[256,512]{1,0:T(8,128)(2,1)} %constant_dynamic-slice_fusion.1), channel_id=1, source_target_pairs={{0,16},{16,0},{1,17},{17,1},{2,18},{18,2},{3,19},{19,3},{4,20},{20... | collective-permute-start | bytes 786440 | tf_op jit(solution)/shard_map/ppermute | solution.py:193
  251.3 11.6 %copy-start.7 = (s32[512]{0:T(512)}, s32[512]{0:T(512)S(1)}, u32[]{:S(2)}) copy-start(s32[512]{0:T(512)S(1)} %pad_add_fusion) | copy-start | bytes 6148
  254.0 166.2 %collective-permute-start = (bf16[256,512]{1,0:T(8,128)(2,1)}, bf16[256,512]{1,0:T(8,128)(2,1)S(1)}, u32[]{:S(2)}, u32[]{:S(2)}) collective-permute-start(bf16[256,512]{1,0:T(8,128)(2,1)} %constant_dynamic-slice_fusion), channel_id=1, source_target_pairs={{0,16},{16,0},{1,17},{17,1},{2,18},{18,2},{3,19},{19,3},{4,20},{20... | collective-permute-start | bytes 786440 | tf_op jit(solution)/shard_map/ppermute | solution.py:193
  274.7 1.1 copy-start
  275.8 1.0 copy-start.1
  276.7 0.9 copy-start.2
  277.7 0.9 copy-start.3
  (1 other events, 0.9 us)

commit v6 on v5

--- a/solution.py
+++ b/solution.py
@@ -10,7 +10,7 @@
 
 EARLY = (1, 7, 24)
 LATE = (6, 20, 4, 1, 1)
-NEAR = 1
+NEAR = 2
 UNIT = 64
 BLOCKS = (1024, 512, 256, 128)
 
@@ -179,6 +179,8 @@
     me = lax.axis_index("player")
     features = width * lax.axis_size("feat")
     half, unit = width // 2, width // UNIT
+    late_sizes = [u * unit for u in LATE]
+    late_sizes[-1:] = [late_sizes[-1] // 2] * 2 if unit >= 256 else late_sizes[-1:]
     ring = [[(i, (i + s) % n) for i in range(n)] for s in range(n)]
 
     sent_at = [jnp.where(me + s < n, 0, half) for s in range(n)]
@@ -186,25 +188,26 @@
 
     source = players
 
-    def send(s, start, size):
+    onward = [[(i, i + s) for i in range(n - s)] for s in range(n)]
+
+    def send(s, start, size, pairs):
         nonlocal source
         piece = lax.dynamic_slice(source, (0, start), (rows, size))
         source, piece = lax.optimization_barrier((source, piece))
-        return lax.ppermute(piece, "player", ring[s])
+        return lax.ppermute(piece, "player", pairs[s])
 
     early, late, place = [], [], 0
     for units in EARLY:
         size = units * unit
-        early.append((place, size, [send(s, sent_at[s] + place, size) for s in range(1, n)]))
+        early.append((place, size, [send(s, sent_at[s] + place, size, ring) for s in range(1, n)]))
         place += size
     place = 0
-    for units in LATE:
-        size = units * unit
+    for size in late_sizes:
         late.append(
             (
                 place,
                 size,
-                [send(s, half - sent_at[s] + place, size) for s in range(1, n)],
+                [send(s, half - sent_at[s] + place, size, onward) for s in range(1, n)],
             )
         )
         place += size
@@ -262,7 +265,7 @@
         for k, (place, size, got) in enumerate(pieces):
             block = next(b for b in BLOCKS if size % b == 0 and place % b == 0)
             base = ((start + place) // block).reshape(1).astype(jnp.int32)
-            near = name == "l" and size == block and k >= len(LATE) - NEAR
+            near = name == "l" and size == block and k >= len(late_sizes) - NEAR
             out = update_piece(base, players, slab, got, coeffs, out, size, block, near)
     return out
 

time: 423 us -> 420 us (level)
  waiting for transfers between devices: 242 us -> 222 us
  starting transfers between devices: 25.9 us -> 40.7 us
    ppermute x8 -> x9, waiting for transfers between devices: 216 us -> 200 us  [send(): return lax.ppermute(piece, 'player', pairs[s])]
    ppermute x8 -> x9, starting transfers between devices: 10.6 us -> 25.4 us  [send(): return lax.ppermute(piece, 'player', pairs[s])]
    dynamic_slice x8 -> x9, local copies, waits for them, and re-layouts: 23.9 us -> 25.2 us  [send(): piece = lax.dynamic_slice(source, (0, start), (rows, size))]
    pallas_call x8 -> x9, Pallas kernels: 59.9 us -> 61.2 us  [update_piece(): pl.pallas_call(functools.partial(update_kernel, count), out_shape=jax.Sha...]
  transfers between devices with their start and end apart: 17 -> 18, of which waited for: 10 -> 10; matrix products, arithmetic and copies ran while one was open for 14% -> 16% of each run, Pallas kernels for 17% -> 17%
where the time goes in v6:
time: 420 us; the launch traced here: 418 us
  waiting for transfers between devices  222 us (53%)
  Pallas kernels  72.7 us (17%)
  matrix products  42.1 us (10%)
  starting transfers between devices  40.7 us (10%)
  local copies, waits for them, and re-layouts  34.1 us (8%)
  other arithmetic  5.92 us (1%)
    ppermute x9, waiting for transfers between devices, send(): return lax.ppermute(piece, 'player', pairs[s])  200 us
    pallas_call x9, Pallas kernels, update_piece(): pl.pallas_call(functools.partial(update_kernel, count), out_shape=jax.Sha...  61.2 us
    dot_general x6, matrix products, dot(): lax.dot_general(a, b, (contract, ((), ())), precision=precision, preferre...  42.1 us
    ppermute x9, starting transfers between devices, send(): return lax.ppermute(piece, 'player', pairs[s])  25.4 us
    dynamic_slice x9, local copies, waits for them, and re-layouts, send(): piece = lax.dynamic_slice(source, (0, start), (rows, size))  25.2 us
    ppermute x4, waiting for transfers between devices, scatter_sum(): got = lax.ppermute(send, axis, [(i, i ^ step) for i in range(size)])  11.9 us
    pallas_call x1, Pallas kernels, coefficients_of(): pl.pallas_call(functools.partial(coeff_kernel, rows, features), out_shape...  11.6 us
  transfers between devices with their start and end apart: 18, of which 10 were waited for; matrix products, arithmetic and copies ran while one was open for 16% of the time, Pallas kernels for 17%

profile of v6, /device:TPU:0, one launch (start us, length us, event | category | flops | bytes accessed | tf_op | source)
XLA Modules:
  0.0 418.0 jit_solution(2430847585685440227)
XLA Ops:
  1.0 3.0 constant_dynamic-slice_fusion.9
  3.9 3.0 collective-permute-start.2
  6.9 6.1 %constant_dynamic-slice_fusion.8 = bf16[256,12288]{1,0:T(8,128)(2,1)} fusion(bf16[256,32768]{1,0:T(8,128)(2,1)} %w_ref.13, s32[]{:T(128)S(6)} %select_n.191), kind=kLoop, calls=%fused_computation.52 | loop fusion | bytes 12582916 | tf_op jit(solution)/shard_map/dynamic_slice | solution.py:195
  17.7 5.4 %constant_dynamic-slice_fusion.6 = bf16[256,10240]{1,0:T(8,128)(2,1)} fusion(bf16[256,32768]{1,0:T(8,128)(2,1)} %w_ref.13, s32[]{:T(128)S(6)} %select_n.193), kind=kLoop, calls=%fused_computation.50 | loop fusion | bytes 10485764 | tf_op jit(solution)/shard_map/dynamic_slice | solution.py:195
  30.2 12.9 %fusion.10 = f32[256,256]{1,0:T(8,128)S(1)} fusion(bf16[256,32768]{1,0:T(8,128)(2,1)} %w_ref.13), kind=kOutput, calls=%fused_computation.60 | convolution fusion | flops 4294967296 | bytes 17039360 | tf_op jit(solution)/shard_map/dot_general | solution.py:22
  43.1 10.5 %fusion.11 = f32[256,128]{1,0:T(8,128)S(1)} fusion(bf16[256,32768]{1,0:T(8,128)(2,1)} %w_ref.13, bf16[128,32768]{1,0:T(8,128)(2,1)} %x_ref.13), kind=kOutput, calls=%fused_computation.61 | convolution fusion | flops 2147483648 | bytes 25296896 | tf_op jit(solution)/shard_map/dot_general | solution.py:22
  53.7 8.1 %fusion.12 = f32[128,128]{1,0:T(8,128)S(1)} fusion(bf16[128,32768]{1,0:T(8,128)(2,1)} %x_ref.13), kind=kOutput, calls=%fused_computation.62 | convolution fusion | flops 1073741824 | bytes 8454144 | tf_op jit(solution)/shard_map/dot_general | solution.py:22
  66.0 121.7 %collective-permute-done.3.refs_0_ = bf16[256,12288]{1,0:T(8,128)(2,1)} collective-permute-done((bf16[256,12288]{1,0:T(8,128)(2,1)}, bf16[256,12288]{1,0:T(8,128)(2,1)}, u32[]{:S(2)}, u32[]{:S(2)}) %collective-permute-start.3) | collective-permute-done | bytes 6291488 | tf_op jit(solution)/shard_map/ppermute | solution.py:197
  187.7 6.4 %fusion = f32[256,256]{1,0:T(8,128)S(1)} fusion(bf16[256,12288]{1,0:T(8,128)(2,1)} %collective-permute-done.3.refs_0_, bf16[256,32768]{1,0:T(8,128)(2,1)} %w_ref.13, s32[]{:T(128)S(6)} %select_n.208), kind=kOutput, calls=%fused_computation | convolution fusion | flops 1610612736 | bytes 12845060 | tf_op jit(solution)/shard_map/dot_general | solution.py:22
  198.0 5.2 %collective-permute-done.5 = f32[64,768]{1,0:T(8,128)S(1)} collective-permute-done((f32[64,768]{1,0:T(8,128)S(1)}, f32[64,768]{1,0:T(8,128)S(1)}, u32[]{:S(2)}, u32[]{:S(2)}) %collective-permute-start.5) | collective-permute-done | bytes 196640 | tf_op jit(solution)/shard_map/ppermute | solution.py:41
  208.0 2.9 collective-permute-start.7
  217.2 2.9 collective-permute-start.9
  220.1 3.1 collective-permute-done.9
  225.6 3.6 collective-permute-done.10
  230.9 5.7 %collective-permute-start.16 = (bf16[256,10240]{1,0:T(8,128)(2,1)}, bf16[256,10240]{1,0:T(8,128)(2,1)}, u32[]{:S(2)}, u32[]{:S(2)}) collective-permute-start(bf16[256,10240]{1,0:T(8,128)(2,1)} %constant_dynamic-slice_fusion.6), channel_id=1, source_target_pairs={{0,16},{1,17},{2,18},{3,19},{4,20},{5,21},{6,22},{7,23},{8,24},{9,... | collective-permute-start | bytes 15728648 | tf_op jit(solution)/shard_map/ppermute | solution.py:197
  237.3 4.6 %collective-permute-start.17 = (bf16[256,3072]{1,0:T(8,128)(2,1)}, bf16[256,3072]{1,0:T(8,128)(2,1)}, u32[]{:S(2)}, u32[]{:S(2)}) collective-permute-start(bf16[256,3072]{1,0:T(8,128)(2,1)} %constant_dynamic-slice_fusion.7), channel_id=1, source_target_pairs={{0,16},{1,17},{2,18},{3,19},{4,20},{5,21},{6,22},{7,23},{8,24},{9,... | collective-permute-start | bytes 4718600 | tf_op jit(solution)/shard_map/ppermute | solution.py:197
  257.9 11.6 %coefficients_of.1 = (bf16[512,640]{1,0:T(8,128)(2,1)}, bf16[256,640]{1,0:T(8,128)(2,1)}, f32[512,1]{1,0:T(8,128)}, f32[256,1]{1,0:T(8,128)}) custom-call(f32[640,640]{1,0:T(8,128)} %maximum_maximum_fusion.gram_ref, s32[512,1]{1,0:T(8,128)} %copy.31.down_ref, s32[1,512]{1,0:T(1,128)} %bitcast.52), custom_call_target="tpu_custom_call" | custom-call | flops 5033164800 | bytes 3276800 | tf_op jit(solution)/shard_map/coefficients_of/pallas_call | solution.py:96
  276.0 8.4 %update_piece.10.refs_5_ = bf16[256,32768]{1,0:T(8,128)(2,1)} custom-call(s32[1]{0:T(128)} %bitcast.21.base_ref, bf16[256,32768]{1,0:T(8,128)(2,1)} %w_ref.13, bf16[128,32768]{1,0:T(8,128)(2,1)} %x_ref.13, bf16[256,3584]{1,0:T(8,128)(2,1)} %copy-done.4, bf16[512,640]{1,0:T(8,128)(2,1)S(1)} %copy-done, ...), custom_call_target="tpu_custom_call", output_to_operand_aliasing={{}: (8, {})} | custom-call | flops 3523215360 | bytes 6422528 | tf_op jit(solution)/shard_map/update_piece/pallas_call | solution.py:151
  284.3 18.6 %update_piece.11.refs_5_ = bf16[256,32768]{1,0:T(8,128)(2,1)} custom-call(s32[1]{0:T(128)} %bitcast.20.base_ref, bf16[256,32768]{1,0:T(8,128)(2,1)} %w_ref.13, bf16[128,32768]{1,0:T(8,128)(2,1)} %x_ref.13, bf16[256,12288]{1,0:T(8,128)(2,1)} %collective-permute-done.3.refs_0_, bf16[512,640]{1,0:T(8,128)(2,1)S(1)} %copy-done, ...), custom_call_target="tpu_custom_call", output_to_operand_aliasing={{}: (8, {})} | custom-call | flops 12079595520 | bytes 22020096 | tf_op jit(solution)/shard_map/update_piece/pallas_call | solution.py:151
  302.9 78.8 %collective-permute-done.17.refs_0_ = bf16[256,3072]{1,0:T(8,128)(2,1)} collective-permute-done((bf16[256,3072]{1,0:T(8,128)(2,1)}, bf16[256,3072]{1,0:T(8,128)(2,1)}, u32[]{:S(2)}, u32[]{:S(2)}) %collective-permute-start.17) | collective-permute-done | bytes 1572896 | tf_op jit(solution)/shard_map/ppermute | solution.py:197
  381.7 4.6 %collective-permute-start = (bf16[256,256]{1,0:T(8,128)(2,1)S(1)}, bf16[256,256]{1,0:T(8,128)(2,1)S(1)}, u32[]{:S(2)}, u32[]{:S(2)}) collective-permute-start(bf16[256,256]{1,0:T(8,128)(2,1)S(1)} %copy-done.7), channel_id=1, source_target_pairs={{0,16},{1,17},{2,18},{3,19},{4,20},{5,21},{6,22},{7,23},{8,24},{9,... | collective-permute-start | bytes 393224 | tf_op jit(solution)/shard_map/ppermute | solution.py:197
  386.3 6.1 %update_piece.12.refs_5_ = bf16[256,32768]{1,0:T(8,128)(2,1)} custom-call(s32[1]{0:T(128)} %bitcast.19.base_ref, bf16[256,32768]{1,0:T(8,128)(2,1)} %w_ref.13, bf16[128,32768]{1,0:T(8,128)(2,1)} %x_ref.13, bf16[256,3072]{1,0:T(8,128)(2,1)} %collective-permute-done.17.refs_0_, bf16[512,640]{1,0:T(8,128)(2,1)S(1)} %copy-done, ...), custom_call_target="tpu_custom_call", output_to_operand_aliasing={{}: (8, {})} | custom-call | flops 3019898880 | bytes 5505024 | tf_op jit(solution)/shard_map/update_piece/pallas_call | solution.py:151
  392.4 15.8 %update_piece.13.refs_5_ = bf16[256,32768]{1,0:T(8,128)(2,1)} custom-call(s32[1]{0:T(128)} %bitcast.18.base_ref, bf16[256,32768]{1,0:T(8,128)(2,1)} %w_ref.13, bf16[128,32768]{1,0:T(8,128)(2,1)} %x_ref.13, bf16[256,10240]{1,0:T(8,128)(2,1)} %collective-permute-done.16.refs_0_, bf16[512,640]{1,0:T(8,128)(2,1)S(1)} %copy-done, ...), custom_call_target="tpu_custom_call", output_to_operand_aliasing={{}: (8, {})} | custom-call | flops 10066329600 | bytes 18350080 | tf_op jit(solution)/shard_map/update_piece/pallas_call | solution.py:151
  408.2 4.6 %update_piece.14.refs_5_ = bf16[256,32768]{1,0:T(8,128)(2,1)} custom-call(s32[1]{0:T(128)} %bitcast.17.base_ref, bf16[256,32768]{1,0:T(8,128)(2,1)} %w_ref.13, bf16[128,32768]{1,0:T(8,128)(2,1)} %x_ref.13, bf16[256,2048]{1,0:T(8,128)(2,1)} %collective-permute-done.15.refs_0_, bf16[512,640]{1,0:T(8,128)(2,1)S(1)} %copy-done, ...), custom_call_target="tpu_custom_call", output_to_operand_aliasing={{}: (8, {})} | custom-call | flops 2013265920 | bytes 3670016 | tf_op jit(solution)/shard_map/update_piece/pallas_call | solution.py:151
  (92 shorter events, 64.2 us)
Async XLA Ops:
  3.9 59.2 %collective-permute-start.2 = (bf16[256,3584]{1,0:T(8,128)(2,1)}, bf16[256,3584]{1,0:T(8,128)(2,1)S(1)}, u32[]{:S(2)}, u32[]{:S(2)}) collective-permute-start(bf16[256,3584]{1,0:T(8,128)(2,1)} %constant_dynamic-slice_fusion.9), channel_id=1, source_target_pairs={{0,16},{16,0},{1,17},{17,1},{2,18},{18,2},{3,19},{19,3},{4,20},{20... | collective-permute-start | bytes 5505032 | tf_op jit(solution)/shard_map/ppermute | solution.py:197
  6.9 54.9 %collective-permute-start.1 = (bf16[256,512]{1,0:T(8,128)(2,1)S(1)}, bf16[256,512]{1,0:T(8,128)(2,1)S(1)}, u32[]{:S(2)}, u32[]{:S(2)}) collective-permute-start(bf16[256,512]{1,0:T(8,128)(2,1)S(1)} %constant_dynamic-slice_fusion.10), channel_id=1, source_target_pairs={{0,16},{16,0},{1,17},{17,1},{2,18},{18,2},{3,19},{19,3},{4,20},{20... | collective-permute-start | bytes 786440 | tf_op jit(solution)/shard_map/ppermute | solution.py:197
  13.1 174.6 %collective-permute-start.3 = (bf16[256,12288]{1,0:T(8,128)(2,1)}, bf16[256,12288]{1,0:T(8,128)(2,1)}, u32[]{:S(2)}, u32[]{:S(2)}) collective-permute-start(bf16[256,12288]{1,0:T(8,128)(2,1)} %constant_dynamic-slice_fusion.8), channel_id=1, source_target_pairs={{0,16},{16,0},{1,17},{17,1},{2,18},{18,2},{3,19},{19,3},{4,20},{20... | collective-permute-start | bytes 18874376 | tf_op jit(solution)/shard_map/ppermute | solution.py:197
  61.8 132.3 %copy-start.5 = (bf16[256,512]{1,0:T(8,128)(2,1)}, bf16[256,512]{1,0:T(8,128)(2,1)S(1)}, u32[]{:S(2)}) copy-start(bf16[256,512]{1,0:T(8,128)(2,1)S(1)} %collective-permute-done.1.refs_0_) | copy-start | bytes 786436
  63.1 131.0 %copy-start.4 = (bf16[256,3584]{1,0:T(8,128)(2,1)}, bf16[256,3584]{1,0:T(8,128)(2,1)S(1)}, u32[]{:S(2)}) copy-start(bf16[256,3584]{1,0:T(8,128)(2,1)S(1)} %collective-permute-done.2.refs_0_) | copy-start | bytes 5505028
  194.3 1.8 collective-permute-start.4
  196.2 7.0 %collective-permute-start.5 = (f32[64,768]{1,0:T(8,128)S(1)}, f32[64,768]{1,0:T(8,128)S(1)}, u32[]{:S(2)}, u32[]{:S(2)}) collective-permute-start(f32[64,768]{1,0:T(8,128)S(1)} %slice_select_fusion.1), channel_id=1, source_target_pairs={{0,2},{1,3},{2,0},{3,1},{4,6},{5,7},{6,4},{7,5},{8,10},{9,11},{10,... | collective-permute-start | bytes 589832 | tf_op jit(solution)/shard_map/ppermute | solution.py:41
  203.3 4.7 %collective-permute-start.6 = (f32[32,768]{1,0:T(8,128)S(1)}, f32[32,768]{1,0:T(8,128)S(1)}, u32[]{:S(2)}, u32[]{:S(2)}) collective-permute-start(f32[32,768]{1,0:T(8,128)S(1)} %slice_select_fusion.2), channel_id=1, source_target_pairs={{0,4},{1,5},{2,6},{3,7},{4,0},{5,1},{6,2},{7,3},{8,12},{9,13},{10,... | collective-permute-start | bytes 294920 | tf_op jit(solution)/shard_map/ppermute | solution.py:41
  208.0 5.1 %collective-permute-start.7 = (f32[16,768]{1,0:T(8,128)S(1)}, f32[16,768]{1,0:T(8,128)S(1)}, u32[]{:S(2)}, u32[]{:S(2)}) collective-permute-start(f32[16,768]{1,0:T(8,128)S(1)} %slice_select_fusion.3), channel_id=1, source_target_pairs={{0,8},{1,9},{2,10},{3,11},{4,12},{5,13},{6,14},{7,15},{8,0},{9,1},... | collective-permute-start | bytes 147464 | tf_op jit(solution)/shard_map/ppermute | solution.py:41
  213.0 4.2 collective-permute-start.8
  217.2 6.0 %collective-permute-start.9 = (f32[2,16,768]{2,1,0:T(8,128)S(1)}, f32[2,16,768]{2,1,0:T(8,128)S(1)}, u32[]{:S(2)}, u32[]{:S(2)}) collective-permute-start(f32[2,16,768]{2,1,0:T(8,128)S(1)} %pad_maximum_fusion.10), channel_id=1, source_target_pairs={{0,8},{1,9},{2,10},{3,11},{4,12},{5,13},{6,14},{7,15},{8,0},{9,1},... | collective-permute-start | bytes 294920 | tf_op jit(solution)/shard_map/ppermute | solution.py:52
  223.2 6.0 %collective-permute-start.10 = (f32[2,32,768]{2,1,0:T(8,128)S(1)}, f32[2,32,768]{2,1,0:T(8,128)S(1)}, u32[]{:S(2)}, u32[]{:S(2)}) collective-permute-start(f32[2,32,768]{2,1,0:T(8,128)S(1)} %pad_maximum_fusion.7), channel_id=1, source_target_pairs={{0,4},{1,5},{2,6},{3,7},{4,0},{5,1},{6,2},{7,3},{8,12},{9,13},{10,... | collective-permute-start | bytes 589832 | tf_op jit(solution)/shard_map/ppermute | solution.py:52
  229.3 7.8 %collective-permute-start.11 = (f32[2,64,768]{2,1,0:T(8,128)S(1)}, f32[2,64,768]{2,1,0:T(8,128)S(1)}, u32[]{:S(2)}, u32[]{:S(2)}) collective-permute-start(f32[2,64,768]{2,1,0:T(8,128)S(1)} %pad_maximum_fusion.2), channel_id=1, source_target_pairs={{0,2},{1,3},{2,0},{3,1},{4,6},{5,7},{6,4},{7,5},{8,10},{9,11},{10,... | collective-permute-start | bytes 1179656 | tf_op jit(solution)/shard_map/ppermute | solution.py:52
  230.9 161.6 %collective-permute-start.16 = (bf16[256,10240]{1,0:T(8,128)(2,1)}, bf16[256,10240]{1,0:T(8,128)(2,1)}, u32[]{:S(2)}, u32[]{:S(2)}) collective-permute-start(bf16[256,10240]{1,0:T(8,128)(2,1)} %constant_dynamic-slice_fusion.6), channel_id=1, source_target_pairs={{0,16},{1,17},{2,18},{3,19},{4,20},{5,21},{6,22},{7,23},{8,24},{9,... | collective-permute-start | bytes 15728648 | tf_op jit(solution)/shard_map/ppermute | solution.py:197
  237.3 11.7 %collective-permute-start.12 = (f32[2,128,768]{2,1,0:T(8,128)S(1)}, f32[2,128,768]{2,1,0:T(8,128)S(1)}, u32[]{:S(2)}, u32[]{:S(2)}) collective-permute-start(f32[2,128,768]{2,1,0:T(8,128)S(1)} %pad_maximum_fusion), channel_id=1, source_target_pairs={{0,1},{1,0},{2,3},{3,2},{4,5},{5,4},{6,7},{7,6},{8,9},{9,8},{10,11... | collective-permute-start | bytes 2359304 | tf_op jit(solution)/shard_map/ppermute | solution.py:52
  237.3 144.4 %collective-permute-start.17 = (bf16[256,3072]{1,0:T(8,128)(2,1)}, bf16[256,3072]{1,0:T(8,128)(2,1)}, u32[]{:S(2)}, u32[]{:S(2)}) collective-permute-start(bf16[256,3072]{1,0:T(8,128)(2,1)} %constant_dynamic-slice_fusion.7), channel_id=1, source_target_pairs={{0,16},{1,17},{2,18},{3,19},{4,20},{5,21},{6,22},{7,23},{8,24},{9,... | collective-permute-start | bytes 4718600 | tf_op jit(solution)/shard_map/ppermute | solution.py:197
  241.9 166.3 %collective-permute-start.15 = (bf16[256,2048]{1,0:T(8,128)(2,1)}, bf16[256,2048]{1,0:T(8,128)(2,1)}, u32[]{:S(2)}, u32[]{:S(2)}) collective-permute-start(bf16[256,2048]{1,0:T(8,128)(2,1)} %constant_dynamic-slice_fusion.5), channel_id=1, source_target_pairs={{0,16},{1,17},{2,18},{3,19},{4,20},{5,21},{6,22},{7,23},{8,24},{9,... | collective-permute-start | bytes 3145736 | tf_op jit(solution)/shard_map/ppermute | solution.py:197
  244.2 168.7 %collective-permute-start.14 = (bf16[256,512]{1,0:T(8,128)(2,1)}, bf16[256,512]{1,0:T(8,128)(2,1)}, u32[]{:S(2)}, u32[]{:S(2)}) collective-permute-start(bf16[256,512]{1,0:T(8,128)(2,1)} %constant_dynamic-slice_fusion.4), channel_id=1, source_target_pairs={{0,16},{1,17},{2,18},{3,19},{4,20},{5,21},{6,22},{7,23},{8,24},{9,... | collective-permute-start | bytes 786440 | tf_op jit(solution)/shard_map/ppermute | solution.py:197
  246.2 11.8 %copy-start.8 = (s32[512]{0:T(512)}, s32[512]{0:T(512)S(1)}, u32[]{:S(2)}) copy-start(s32[512]{0:T(512)S(1)} %pad_add_fusion) | copy-start | bytes 6148
  249.8 165.6 %collective-permute-start.13 = (bf16[256,256]{1,0:T(8,128)(2,1)}, bf16[256,256]{1,0:T(8,128)(2,1)S(1)}, u32[]{:S(2)}, u32[]{:S(2)}) collective-permute-start(bf16[256,256]{1,0:T(8,128)(2,1)} %constant_dynamic-slice_fusion.3), channel_id=1, source_target_pairs={{0,16},{1,17},{2,18},{3,19},{4,20},{5,21},{6,22},{7,23},{8,24},{9,... | collective-permute-start | bytes 393224 | tf_op jit(solution)/shard_map/ppermute | solution.py:197
  269.5 1.1 copy-start
  270.6 1.0 copy-start.1
  284.3 97.4 %copy-start.7 = (bf16[256,256]{1,0:T(8,128)(2,1)S(1)}, bf16[256,256]{1,0:T(8,128)(2,1)}, u32[]{:S(2)}) copy-start(bf16[256,256]{1,0:T(8,128)(2,1)} %constant_dynamic-slice_fusion.2) | copy-start | bytes 393220
  381.7 35.0 %collective-permute-start = (bf16[256,256]{1,0:T(8,128)(2,1)S(1)}, bf16[256,256]{1,0:T(8,128)(2,1)S(1)}, u32[]{:S(2)}, u32[]{:S(2)}) collective-permute-start(bf16[256,256]{1,0:T(8,128)(2,1)S(1)} %copy-done.7), channel_id=1, source_target_pairs={{0,16},{1,17},{2,18},{3,19},{4,20},{5,21},{6,22},{7,23},{8,24},{9,... | collective-permute-start | bytes 393224 | tf_op jit(solution)/shard_map/ppermute | solution.py:197
  (3 other events, 2.7 us)
